TPU v7x, 32 devices: a whole 2x2x4 slice. The times are simulated.
32 devices in a mesh: row: 4 (over y, core), col: 8 (over z, x).
Axes of the slice: x: 2, y: 2, z: 4, core: 2. Of those that a mesh axis runs over, the one named last changes fastest.
Arguments:
- coarse_feats: bfloat16 [8192, 512], P(('row', 'col')), may hold values from -6 to 6
- fine_feats: bfloat16 [32768, 256], P(('row', 'col')), may hold values from -6 to 6
- parent_index: int32 [32768], P(('row', 'col')), may hold values from 0 to 8191, as said below
- nbr_offset: int32 [27, 32768], P(None, ('row', 'col')), may hold values from -256 to 257, as said below
- z_position: int32 [32768], P(('row', 'col')), may hold values from 0 to 32767, as said below
- segment_id: int32 [32768], P(('row', 'col')), may hold values from 0 to 63, never falling along the last dimension, each value on 1 to 2048 neighbouring positions
- w_parent: bfloat16 [512, 256], replicated, may hold values from -0.25 to 0.25
- w_skip: bfloat16 [256, 256], replicated, may hold values from -0.375 to 0.375
- conv_taps: float32 [27, 256], replicated, may hold values from -1.5 to 1.5
- w_cpe: bfloat16 [256, 256], replicated, may hold values from -0.375 to 0.375
- w_qkv: bfloat16 [256, 768], replicated
- w_out: bfloat16 [256, 256], replicated, may hold values from -0.375 to 0.375
- w_up: bfloat16 [256, 1024], replicated, may hold values from -0.375 to 0.375
- w_down: bfloat16 [1024, 256], replicated, may hold values from -0.1875 to 0.1875
- w_cls: bfloat16 [13, 256], replicated, may hold values from -0.375 to 0.375
Outputs:
- logits: float32 [13, 32768], P(None, ('row', 'col'))
Inputs may be any that keep to these rules, and one draw needn't show every extreme that they name: parent_index[g] differs from g // 4 by at most 128; it is that far below at the first point of every device's shard and that far above at the last, where the grid allows. `nbr_offset`: the offset for kernel position 13 is 0; present neighbours lie inside the grid; the first kernel offset of each shard's first point is -256 and the last offset of each shard's last point is 256, where the grid allows. `z_position`: a permutation; at most 64 of one device's 1024 points have z positions in one device's block of 1024 consecutive z positions, and exactly 64 for some pairs of devices.
All inputs are finite; a program needn't handle non-finite values.
Results may differ from a plain program's by a relative error of at most 0.014.
The roundings to bfloat16 on the way count: a program that leaves them out, or rounds other values in their place, can miss the bound.
Values may be sent and summed in bfloat16 or wider, within the bound.
A program may use at most 64 MiB of HBM per device.

v0:
```python
import math

import jax
import jax.numpy as jnp
from jax import lax
from jax.sharding import PartitionSpec as P

HEADS = 16
PATCH = 1024
REACH = 256


def padded(cells, sides, width):
    for axis, dim in sides:
        count = lax.axis_size(axis)
        ends = count - 1
        head = lax.slice_in_dim(cells, 0, width, axis=dim)
        tail = lax.slice_in_dim(cells, cells.shape[dim] - width, cells.shape[dim], axis=dim)
        cells = jnp.concatenate(
            [
                lax.ppermute(tail, axis, [(i, (i + 1) % count) for i in range(ends)]),
                cells,
                lax.ppermute(head, axis, [((i + 1) % count, i) for i in range(ends)]),
            ],
            axis=dim,
        )
    return cells


def layer_norm(values):
    center = values - jnp.mean(values, axis=-1, keepdims=True)
    spread = jnp.mean(center * center, axis=-1, keepdims=True)
    return center * lax.rsqrt(spread + 1e-05)


def attend_local(z_feats, seg_local, w_qkv, w_out):
    total_rows, feat_width = z_feats.shape
    head_dim = feat_width // HEADS
    group_size = math.gcd(HEADS, 4)
    scale_factor = head_dim ** (-0.5)
    normed = layer_norm(z_feats.astype(jnp.float32)).astype(jnp.bfloat16)
    qkv_all = jnp.dot(normed, w_qkv, preferred_element_type=jnp.float32).astype(jnp.bfloat16)

    def one_patch(start):
        same_seg = seg_local[:, None] == seg_local[None, :]
        split = qkv_all.reshape(PATCH, 3, HEADS // group_size, group_size, head_dim)
        split = jnp.transpose(split, (1, 2, 3, 0, 4))

        def one_group(operands):
            queries, key_rows, value_rows = operands
            scores = (
                jnp.einsum("hqd,hkd->hqk", queries, key_rows, preferred_element_type=jnp.float32)
                * scale_factor
            )
            scores = jnp.where(same_seg[None], scores, -1e30)
            row_max = jnp.max(scores, axis=-1, keepdims=True)
            exp_scores = jnp.exp(scores - row_max)
            probs = (exp_scores / jnp.sum(exp_scores, axis=-1, keepdims=True)).astype(jnp.bfloat16)
            return jnp.einsum(
                "hqk,hkd->hqd", probs, value_rows, preferred_element_type=jnp.float32
            ).astype(jnp.bfloat16)

        grouped = lax.map(one_group, (split[0], split[1], split[2]))
        return jnp.transpose(grouped, (2, 0, 1, 3)).reshape(PATCH, feat_width)

    starts = jnp.arange(total_rows // PATCH, dtype=jnp.int32) * PATCH
    att = lax.map(one_patch, starts).reshape(total_rows, feat_width)
    return jnp.dot(att, w_out, preferred_element_type=jnp.float32).astype(jnp.bfloat16)


def point_head(x_feats, att_out, w_up, w_down, w_cls):
    x_two = x_feats.astype(jnp.float32) + att_out.astype(jnp.float32)
    hidden = jax.nn.gelu(
        jnp.dot(layer_norm(x_two).astype(jnp.bfloat16), w_up, preferred_element_type=jnp.float32)
    ).astype(jnp.bfloat16)
    x_three = x_two + jnp.dot(hidden, w_down, preferred_element_type=jnp.float32)
    final_norm = layer_norm(x_three).astype(jnp.bfloat16)
    return lax.dot_general(
        w_cls, final_norm, (((1,), (1,)), ((), ())), preferred_element_type=jnp.float32
    )


def local(
    coarse_feats,
    fine_feats,
    parent_index,
    nbr_offset,
    z_position,
    segment_id,
    w_parent,
    w_skip,
    conv_taps,
    w_cpe,
    w_qkv,
    w_out,
    w_up,
    w_down,
    w_cls,
):
    fine_rows, feat_width = fine_feats.shape
    coarse_rows = coarse_feats.shape[0]
    devices = lax.axis_size(("row", "col"))
    dev_index = lax.axis_index(("row", "col"))
    parent_local = jax.nn.gelu(
        layer_norm(jnp.dot(coarse_feats, w_parent, preferred_element_type=jnp.float32))
    ).astype(jnp.bfloat16)
    margin = coarse_rows // 2
    parent_ext = padded(parent_local, ((("row", "col"), 0),), margin)
    parent_rows = parent_index - (dev_index * coarse_rows - margin)
    parent_pick = (
        parent_rows[:, None] == jnp.arange(parent_ext.shape[0], dtype=jnp.int32)[None, :]
    ).astype(jnp.bfloat16)
    parents = jnp.dot(parent_pick, parent_ext, preferred_element_type=jnp.float32)
    skip = jax.nn.gelu(layer_norm(jnp.dot(fine_feats, w_skip, preferred_element_type=jnp.float32)))
    feat = (parents + skip).astype(jnp.bfloat16)
    depth = REACH
    feat_ext = padded(feat, ((("row", "col"), 0),), depth)
    block_rows = min(512, fine_rows)
    window = block_rows + 2 * depth
    local_rows = jnp.arange(block_rows, dtype=jnp.int32) + depth
    window_cols = jnp.arange(window, dtype=jnp.int32)

    def conv_block(block_start):
        window_rows = lax.dynamic_slice_in_dim(feat_ext, block_start, window, 0)
        block_offsets = lax.dynamic_slice_in_dim(nbr_offset, block_start, block_rows, 1)

        def add_tap(tap_index, running):
            offsets = lax.dynamic_index_in_dim(block_offsets, tap_index, 0, keepdims=False)
            weights = lax.dynamic_index_in_dim(conv_taps, tap_index, 0, keepdims=False)
            present = offsets != REACH + 1
            source = jnp.where(present, local_rows + offsets, -1)
            picker = (source[:, None] == window_cols[None, :]).astype(jnp.bfloat16)
            gathered = jnp.dot(picker, window_rows, preferred_element_type=jnp.float32)
            return running + gathered * weights[None, :]

        total = lax.fori_loop(
            0, nbr_offset.shape[0], add_tap, jnp.zeros((block_rows, feat_width), jnp.float32)
        )
        return total.astype(jnp.bfloat16)

    block_starts = jnp.arange(fine_rows // block_rows, dtype=jnp.int32) * block_rows
    conv = lax.map(conv_block, block_starts).reshape(fine_rows, feat_width)
    x_feats = (
        feat.astype(jnp.float32)
        + layer_norm(jnp.dot(conv, w_cpe, preferred_element_type=jnp.float32))
    ).astype(jnp.bfloat16)
    capacity = 2 * fine_rows // devices
    dest_dev = z_position // fine_rows
    z_slot = z_position % fine_rows
    one_hot = (dest_dev[:, None] == jnp.arange(devices, dtype=jnp.int32)[None, :]).astype(jnp.int32)
    rank_in = jnp.sum(jnp.cumsum(one_hot, axis=0) * one_hot, axis=1) - 1
    buffer_pos = dest_dev * capacity + rank_in
    send_feats = (
        jnp.zeros((devices * capacity, feat_width), jnp.bfloat16).at[buffer_pos].set(x_feats)
    )
    send_slots = jnp.full((devices * capacity,), -1, jnp.int32).at[buffer_pos].set(z_slot)
    recv_feats, recv_slots = (
        lax.all_to_all(
            send_feats.reshape(devices, capacity, feat_width),
            ("row", "col"),
            split_axis=0,
            concat_axis=0,
            tiled=True,
        ),
        lax.all_to_all(
            send_slots.reshape(devices, capacity),
            ("row", "col"),
            split_axis=0,
            concat_axis=0,
            tiled=True,
        ),
    )
    recv_feats = recv_feats.reshape(devices * capacity, feat_width)
    recv_slots = recv_slots.reshape(devices * capacity)
    target_slot = jnp.where(recv_slots >= 0, recv_slots, fine_rows)
    z_feats = (
        jnp.zeros((fine_rows, feat_width), jnp.bfloat16)
        .at[target_slot]
        .set(recv_feats, mode="drop")
    )
    att_out = attend_local(z_feats, segment_id, w_qkv, w_out)
    back_index = jnp.minimum(target_slot, fine_rows - 1)
    back_feats = jnp.take(att_out, back_index, axis=0)
    returned = lax.all_to_all(
        back_feats.reshape(devices, capacity, feat_width),
        ("row", "col"),
        split_axis=0,
        concat_axis=0,
        tiled=True,
    )
    att_home = jnp.take(returned.reshape(devices * capacity, feat_width), buffer_pos, axis=0)
    return point_head(x_feats, att_home, w_up, w_down, w_cls)


def solution(mesh):
    placed = (
        P(("row", "col"), None),
        P(("row", "col"), None),
        P(("row", "col")),
        P(None, ("row", "col")),
        P(("row", "col")),
        P(("row", "col")),
        P(),
        P(),
        P(),
        P(),
        P(),
        P(),
        P(),
        P(),
        P(),
    )
    return jax.shard_map(
        local, mesh=mesh, in_specs=placed, out_specs=P(None, ("row", "col")), check_vma=False
    )
```

profile of v0, /device:TPU:0, one launch (start us, length us, event | category | flops | bytes accessed | tf_op | source)
XLA Modules:
  0.0 303.7 jit_solution(6786620721431900635)
XLA Ops:
  1.6 4.9 %collective-permute-start = (bf16[128,256]{0,1:T(8,128)(2,1)S(1)}, bf16[128,256]{0,1:T(8,128)(2,1)S(1)}, u32[]{:S(2)}, u32[]{:S(2)}) collective-permute-start(bf16[128,256]{0,1:T(8,128)(2,1)S(1)} %get-tuple-element.350), channel_id=1, source_target_pairs={{0,1},{1,2},{2,3},{3,4},{4,5},{5,6},{6,7},{7,8},{8,9},{9,10},{10,1... | collective-permute-start | bytes 196616 | tf_op jit(solution)/shard_map/ppermute | solution.py:21
  8.5 9.0 %reduce-window.6 = s32[32,8,128]{2,1,0:T(8,128)S(1)} reduce-window(s32[32,8,128]{2,1,0:T(8,128)S(1)} %fusion.111, s32[]{:T(128)} %copy.65), window={size=1x1x128 pad=0_0x0_0x127_0}, to_apply=%region_10.11 | reduce-window | flops 4161536 | bytes 262148 | tf_op jit(solution)/shard_map/reduce-window
  20.5 4.6 %collective-permute-start.2 = (bf16[256,256]{0,1:T(8,128)(2,1)S(1)}, bf16[256,256]{0,1:T(8,128)(2,1)S(1)}, u32[]{:S(2)}, u32[]{:S(2)}) collective-permute-start(bf16[256,256]{0,1:T(8,128)(2,1)S(1)} %get-tuple-element.348), channel_id=1, source_target_pairs={{0,1},{1,2},{2,3},{3,4},{4,5},{5,6},{6,7},{7,8},{8,9},{9,10},{10,1... | collective-permute-start | bytes 393224 | tf_op jit(solution)/shard_map/ppermute | solution.py:21
  27.0 4.3 %scatter_custom_fusion = s32[2048]{0:T(1024)S(1)} fusion(s32[1024]{0:T(1024)S(1)} %get-tuple-element.342, s32[1024]{0:T(1024)S(1)} %get-tuple-element.354, s32[]{:T(128)} %constant.205.clone.1), kind=kCustom, calls=%fused_computation.149 | custom fusion | bytes 8196 | tf_op jit(solution)/shard_map/scatter | solution.py:156
  32.0 9.7 %all-to-all-start = ((s32[32,1,64]{2,1,0:T(1,128)}), s32[32,1,64]{2,1,0:T(1,128)S(1)}, u32[]{:S(2)}, u32[]{:S(2)}) async-start(s32[32,1,64]{2,1,0:T(1,128)} %all_to_all.12), calls=%async_computation | async-start | bytes 32768 | tf_op jit(solution)/shard_map/all_to_all | solution.py:165
  41.8 85.5 %while.45 = (s32[]{:T(128)}, bf16[2,512,256]{2,1,0:T(8,128)(2,1)}, s32[2]{0:T(128)S(1)}, s32[27,1024]{1,0:T(8,128)S(1)}, bf16[1536,256]{0,1:T(8,128)(2,1)S(1)}, ...) while((s32[]{:T(128)}, bf16[2,512,256]{2,1,0:T(8,128)(2,1)}, ...), condition=%wide.region_7.8_spmd.clone, body=%wide.region_4.7_spmd.clone.sunk | while | flops 269486080 | bytes 4593047 | solution.py:142
  46.2 37.6 %while.47 = (s32[]{:T(128)}, f32[512,256]{1,0:T(8,128)S(1)}, s32[27,512]{1,0:T(8,128)S(1)}, s32[512]{0:T(512)S(1)}, s32[1024]{0:T(1024)S(1)}, /*index=5*/bf16[10...) while((s32[]{:T(128)}, f32[512,256]{1,0:T(8,128)S(1)}, s32[27,512]{1,0:T(8,128)S(1)}, ...), condition=%wide.region_6.6_spmd.clone, body=%wide.region_5.5_spmd.clone.sunk | while | flops 269354496 | bytes 1592439 | solution.py:136
  88.9 37.6 %while.47 = (s32[]{:T(128)}, f32[512,256]{1,0:T(8,128)S(1)}, s32[27,512]{1,0:T(8,128)S(1)}, s32[512]{0:T(512)S(1)}, s32[1024]{0:T(1024)S(1)}, /*index=5*/bf16[10...) while((s32[]{:T(128)}, f32[512,256]{1,0:T(8,128)S(1)}, s32[27,512]{1,0:T(8,128)S(1)}, ...), condition=%wide.region_6.6_spmd.clone, body=%wide.region_5.5_spmd.clone.sunk | while | flops 269354496 | bytes 1592439 | solution.py:136
  129.2 6.0 %scatter_custom_fusion.1 = bf16[2048,256]{1,0:T(8,128)(2,1)} fusion(s32[1024]{0:T(1024)S(1)} %get-tuple-element.342, bf16[1024,256]{1,0:T(8,128)(2,1)S(1)} %copy.35, bf16[]{:T(256)} %constant.200.clone.1), kind=kCustom, calls=%fused_computation.104 | custom fusion | bytes 1048578 | tf_op jit(solution)/shard_map/scatter | solution.py:154
  135.2 5.8 %all-to-all-start.1 = ((bf16[32,64,256]{2,1,0:T(8,128)(2,1)}), bf16[32,64,256]{2,1,0:T(8,128)(2,1)S(1)}, u32[]{:S(2)}, u32[]{:S(2)}) async-start(bf16[32,64,256]{2,1,0:T(8,128)(2,1)} %bitcast.6), calls=%async_computation.1 | async-start | bytes 2097152 | tf_op jit(solution)/shard_map/all_to_all | solution.py:158
  142.4 26.1 %all-to-all-done.1 = bf16[32,64,256]{2,1,0:T(8,128)(2,1)S(1)} async-done(((bf16[32,64,256]{2,1,0:T(8,128)(2,1)}), bf16[32,64,256]{2,1,0:T(8,128)(2,1)S(1)}, u32[]{:S(2)}, u32[]{:S(2)}) %all-to-all-start.1) | async-done | bytes 1048608 | tf_op jit(solution)/shard_map/all_to_all | solution.py:158
  168.5 9.5 %scatter_custom_fusion.2 = bf16[1024,256]{1,0:T(8,128)(2,1)S(1)} fusion(s32[2048]{0:T(1024)S(1)} %bitcast.120, bf16[2048,256]{1,0:T(8,128)(2,1)S(1)} %bitcast.111, bf16[]{:T(256)} %constant.200.clone.1), kind=kCustom, calls=%fused_computation.122 | custom fusion | bytes 524290 | tf_op jit(solution)/shard_map/scatter | solution.py:179
  181.8 73.5 %while.46 = (s32[]{:T(128)}, bf16[4,4,1024,16]{2,3,1,0:T(8,128)(2,1)S(1)}, bf16[4,4,1024,16]{2,3,1,0:T(8,128)(2,1)}, bf16[4,4,1024,16]{2,3,1,0:T(8,128)(2,1)}, b...) while((s32[]{:T(128)}, bf16[4,4,1024,16]{2,3,1,0:T(8,128)(2,1)S(1)}, ...), condition=%wide.region_21.22_spmd.clone, body=%wide.region_18.21_spmd.clone.sunk | while | flops 294716416 | bytes 36214868 | solution.py:63
  182.4 10.7 %fusion.163 = (f32[4,1024]{1,0:T(4,128)S(1)}, f32[4,1024,1024]{1,2,0:T(8,128)}) fusion(pred[1024,1024]{0,1:T(8,128)(4,1)S(1)} %broadcast_compare_fusion.2, bf16[4,4,1024,16]{2,3,1,0:T(8,128)(2,1)} %get-tuple-element.582, s32[]{:T(128)S(6)} %copy.59, bf16[4,4,1024,16]{2,3,1,0:T(8,128)(2,1)} %get-tuple-element.581), kind=kOutput, calls=%fused_computation.173.clone.1 | convolution fusion | flops 150995968 | bytes 18105344 | tf_op jit(solution)/shard_map/while/body/eval_jaxpr/while/body/eval_jaxpr/sub | solution.py:57
  193.2 7.0 %fusion.164 = bf16[4,4,1024,16]{2,3,1,0:T(8,128)(2,1)S(1)} fusion(bf16[4,4,1024,16]{2,3,1,0:T(8,128)(2,1)S(1)} %get-tuple-element.573, s32[]{:T(128)S(6)} %copy.59, f32[4,1024,1024]{1,2,0:T(8,128)} %get-tuple-element.493, f32[4,1024]{1,0:T(4,128)S(1)} %get-tuple-element.494, bf16[4,4,1024,16]{2,3,1,0:T(8,128)(2,1)S(1)} %get-tuple-element.583), kind=kOutput, calls=%fused_computation.21.clone.1 | convolution fusion | flops 142671872 | bytes 17056768 | tf_op jit(solution)/shard_map/while/body/eval_jaxpr/while/body/eval_jaxpr/hqk,hkd->hqd/dot_general | solution.py:59
  200.8 10.7 %fusion.163 = (f32[4,1024]{1,0:T(4,128)S(1)}, f32[4,1024,1024]{1,2,0:T(8,128)}) fusion(pred[1024,1024]{0,1:T(8,128)(4,1)S(1)} %broadcast_compare_fusion.2, bf16[4,4,1024,16]{2,3,1,0:T(8,128)(2,1)} %get-tuple-element.582, s32[]{:T(128)S(6)} %copy.59, bf16[4,4,1024,16]{2,3,1,0:T(8,128)(2,1)} %get-tuple-element.581), kind=kOutput, calls=%fused_computation.173.clone.1 | convolution fusion | flops 150995968 | bytes 18105344 | tf_op jit(solution)/shard_map/while/body/eval_jaxpr/while/body/eval_jaxpr/sub | solution.py:57
  211.5 7.0 %fusion.164 = bf16[4,4,1024,16]{2,3,1,0:T(8,128)(2,1)S(1)} fusion(bf16[4,4,1024,16]{2,3,1,0:T(8,128)(2,1)S(1)} %get-tuple-element.573, s32[]{:T(128)S(6)} %copy.59, f32[4,1024,1024]{1,2,0:T(8,128)} %get-tuple-element.493, f32[4,1024]{1,0:T(4,128)S(1)} %get-tuple-element.494, bf16[4,4,1024,16]{2,3,1,0:T(8,128)(2,1)S(1)} %get-tuple-element.583), kind=kOutput, calls=%fused_computation.21.clone.1 | convolution fusion | flops 142671872 | bytes 17056768 | tf_op jit(solution)/shard_map/while/body/eval_jaxpr/while/body/eval_jaxpr/hqk,hkd->hqd/dot_general | solution.py:59
  219.2 10.7 %fusion.163 = (f32[4,1024]{1,0:T(4,128)S(1)}, f32[4,1024,1024]{1,2,0:T(8,128)}) fusion(pred[1024,1024]{0,1:T(8,128)(4,1)S(1)} %broadcast_compare_fusion.2, bf16[4,4,1024,16]{2,3,1,0:T(8,128)(2,1)} %get-tuple-element.582, s32[]{:T(128)S(6)} %copy.59, bf16[4,4,1024,16]{2,3,1,0:T(8,128)(2,1)} %get-tuple-element.581), kind=kOutput, calls=%fused_computation.173.clone.1 | convolution fusion | flops 150995968 | bytes 18105344 | tf_op jit(solution)/shard_map/while/body/eval_jaxpr/while/body/eval_jaxpr/sub | solution.py:57
  229.9 7.0 %fusion.164 = bf16[4,4,1024,16]{2,3,1,0:T(8,128)(2,1)S(1)} fusion(bf16[4,4,1024,16]{2,3,1,0:T(8,128)(2,1)S(1)} %get-tuple-element.573, s32[]{:T(128)S(6)} %copy.59, f32[4,1024,1024]{1,2,0:T(8,128)} %get-tuple-element.493, f32[4,1024]{1,0:T(4,128)S(1)} %get-tuple-element.494, bf16[4,4,1024,16]{2,3,1,0:T(8,128)(2,1)S(1)} %get-tuple-element.583), kind=kOutput, calls=%fused_computation.21.clone.1 | convolution fusion | flops 142671872 | bytes 17056768 | tf_op jit(solution)/shard_map/while/body/eval_jaxpr/while/body/eval_jaxpr/hqk,hkd->hqd/dot_general | solution.py:59
  237.6 10.7 %fusion.163 = (f32[4,1024]{1,0:T(4,128)S(1)}, f32[4,1024,1024]{1,2,0:T(8,128)}) fusion(pred[1024,1024]{0,1:T(8,128)(4,1)S(1)} %broadcast_compare_fusion.2, bf16[4,4,1024,16]{2,3,1,0:T(8,128)(2,1)} %get-tuple-element.582, s32[]{:T(128)S(6)} %copy.59, bf16[4,4,1024,16]{2,3,1,0:T(8,128)(2,1)} %get-tuple-element.581), kind=kOutput, calls=%fused_computation.173.clone.1 | convolution fusion | flops 150995968 | bytes 18105344 | tf_op jit(solution)/shard_map/while/body/eval_jaxpr/while/body/eval_jaxpr/sub | solution.py:57
  248.3 7.0 %fusion.164 = bf16[4,4,1024,16]{2,3,1,0:T(8,128)(2,1)S(1)} fusion(bf16[4,4,1024,16]{2,3,1,0:T(8,128)(2,1)S(1)} %get-tuple-element.573, s32[]{:T(128)S(6)} %copy.59, f32[4,1024,1024]{1,2,0:T(8,128)} %get-tuple-element.493, f32[4,1024]{1,0:T(4,128)S(1)} %get-tuple-element.494, bf16[4,4,1024,16]{2,3,1,0:T(8,128)(2,1)S(1)} %get-tuple-element.583), kind=kOutput, calls=%fused_computation.21.clone.1 | convolution fusion | flops 142671872 | bytes 17056768 | tf_op jit(solution)/shard_map/while/body/eval_jaxpr/while/body/eval_jaxpr/hqk,hkd->hqd/dot_general | solution.py:59
  255.7 7.5 %gather_fusion = bf16[2048,256]{1,0:T(8,128)(2,1)S(1)} fusion(bf16[1024,256]{1,0:T(8,128)(2,1)S(1)} %convolution_convert_fusion.1, s32[2048]{0:T(1024)S(1)} %broadcast_clamp_fusion), kind=kCustom, calls=%fused_computation | custom fusion | bytes 2105344 | tf_op jit(solution)/shard_map/jit(_take)/gather | solution.py:183
  267.2 27.5 %all-to-all-done.2 = bf16[32,64,256]{2,1,0:T(8,128)(2,1)S(1)} async-done(((bf16[32,64,256]{2,1,0:T(8,128)(2,1)}), bf16[32,64,256]{2,1,0:T(8,128)(2,1)S(1)}, u32[]{:S(2)}, u32[]{:S(2)}) %all-to-all-start.2) | async-done | bytes 1048608 | tf_op jit(solution)/shard_map/all_to_all | solution.py:184
  294.7 3.9 %gather_fusion.1 = bf16[1024,256]{1,0:T(8,128)(2,1)S(1)} fusion(bf16[2048,256]{1,0:T(8,128)(2,1)S(1)} %bitcast.107, s32[1024]{0:T(1024)S(1)} %broadcast_clamp_fusion.1), kind=kCustom, calls=%fused_computation.1 | custom fusion | bytes 1052672 | tf_op jit(solution)/shard_map/jit(_take)/gather | solution.py:191
  (321 shorter events, 105.3 us)
Async XLA Ops:
  0.0 18.0 %copy-start = (bf16[1024,256]{1,0:T(8,128)(2,1)S(1)}, bf16[1024,256]{1,0:T(8,128)(2,1)}, u32[]{:S(2)}) copy-start(bf16[1024,256]{1,0:T(8,128)(2,1)} %param.22) | copy-start | bytes 1572868
  0.0 19.4 %copy-start.8 = (s32[1024]{0:T(1024)S(1)}, s32[1024]{0:T(1024)}, u32[]{:S(2)}) copy-start(s32[1024]{0:T(1024)} %param.23) | copy-start | bytes 12292
  1.6 17.9 %collective-permute-start = (bf16[128,256]{0,1:T(8,128)(2,1)S(1)}, bf16[128,256]{0,1:T(8,128)(2,1)S(1)}, u32[]{:S(2)}, u32[]{:S(2)}) collective-permute-start(bf16[128,256]{0,1:T(8,128)(2,1)S(1)} %get-tuple-element.350), channel_id=1, source_target_pairs={{0,1},{1,2},{2,3},{3,4},{4,5},{5,6},{6,7},{7,8},{8,9},{9,10},{10,1... | collective-permute-start | bytes 196616 | tf_op jit(solution)/shard_map/ppermute | solution.py:21
  6.5 13.0 %collective-permute-start.1 = (bf16[128,256]{0,1:T(8,128)(2,1)S(1)}, bf16[128,256]{0,1:T(8,128)(2,1)S(1)}, u32[]{:S(2)}, u32[]{:S(2)}) collective-permute-start(bf16[128,256]{0,1:T(8,128)(2,1)S(1)} %get-tuple-element.351), channel_id=1, source_target_pairs={{1,0},{2,1},{3,2},{4,3},{5,4},{6,5},{7,6},{8,7},{9,8},{10,9},{11,1... | collective-permute-start | bytes 196616 | tf_op jit(solution)/shard_map/ppermute | solution.py:23
  19.3 22.5 %copy-start.1 = (s32[27,1024]{1,0:T(8,128)S(1)}, s32[27,1024]{1,0:T(8,128)}, u32[]{:S(2)}) copy-start(s32[27,1024]{1,0:T(8,128)} %param.24) | copy-start | bytes 331780
  20.5 21.2 %collective-permute-start.2 = (bf16[256,256]{0,1:T(8,128)(2,1)S(1)}, bf16[256,256]{0,1:T(8,128)(2,1)S(1)}, u32[]{:S(2)}, u32[]{:S(2)}) collective-permute-start(bf16[256,256]{0,1:T(8,128)(2,1)S(1)} %get-tuple-element.348), channel_id=1, source_target_pairs={{0,1},{1,2},{2,3},{3,4},{4,5},{5,6},{6,7},{7,8},{8,9},{9,10},{10,1... | collective-permute-start | bytes 393224 | tf_op jit(solution)/shard_map/ppermute | solution.py:21
  25.1 16.6 %collective-permute-start.3 = (bf16[256,256]{0,1:T(8,128)(2,1)S(1)}, bf16[256,256]{0,1:T(8,128)(2,1)S(1)}, u32[]{:S(2)}, u32[]{:S(2)}) collective-permute-start(bf16[256,256]{0,1:T(8,128)(2,1)S(1)} %get-tuple-element.349), channel_id=1, source_target_pairs={{1,0},{2,1},{3,2},{4,3},{5,4},{6,5},{7,6},{8,7},{9,8},{10,9},{11,1... | collective-permute-start | bytes 393224 | tf_op jit(solution)/shard_map/ppermute | solution.py:23
  32.0 103.3 %all-to-all-start = ((s32[32,1,64]{2,1,0:T(1,128)}), s32[32,1,64]{2,1,0:T(1,128)S(1)}, u32[]{:S(2)}, u32[]{:S(2)}) async-start(s32[32,1,64]{2,1,0:T(1,128)} %all_to_all.12), calls=%async_computation | async-start | bytes 32768 | tf_op jit(solution)/shard_map/all_to_all | solution.py:165
  41.7 85.5 %copy-start.5 = (bf16[256,256]{1,0:T(8,128)(2,1)S(1)}, bf16[256,256]{1,0:T(8,128)(2,1)}, u32[]{:S(2)}) copy-start(bf16[256,256]{1,0:T(8,128)(2,1)} %param.30) | copy-start | bytes 393220
  135.2 33.3 %all-to-all-start.1 = ((bf16[32,64,256]{2,1,0:T(8,128)(2,1)}), bf16[32,64,256]{2,1,0:T(8,128)(2,1)S(1)}, u32[]{:S(2)}, u32[]{:S(2)}) async-start(bf16[32,64,256]{2,1,0:T(8,128)(2,1)} %bitcast.6), calls=%async_computation.1 | async-start | bytes 2097152 | tf_op jit(solution)/shard_map/all_to_all | solution.py:158
  141.1 40.7 %copy-start.3 = (s32[1024]{0:T(1024)S(1)}, s32[1024]{0:T(1024)}, u32[]{:S(2)}) copy-start(s32[1024]{0:T(1024)} %param.26) | copy-start | bytes 12292
  178.1 3.7 %copy-start.2 = (bf16[4,4,1024,16]{2,3,1,0:T(8,128)(2,1)S(1)}, bf16[4,4,1024,16]{2,3,1,0:T(8,128)(2,1)}, u32[]{:S(2)}) copy-start(bf16[4,4,1024,16]{2,3,1,0:T(8,128)(2,1)} %custom-call.7) | copy-start | bytes 1572868
  181.8 73.5 %copy-start.4 = (bf16[256,256]{1,0:T(8,128)(2,1)S(1)}, bf16[256,256]{1,0:T(8,128)(2,1)}, u32[]{:S(2)}) copy-start(bf16[256,256]{1,0:T(8,128)(2,1)} %param.32) | copy-start | bytes 393220
  264.4 34.4 %copy-start.6 = (pred[1024]{0:T(1024)(128)(4,1)S(1)}, pred[1024]{0:T(1024)(128)(4,1)}, u32[]{:S(2)}) copy-start(pred[1024]{0:T(1024)(128)(4,1)} %get-tuple-element.341) | copy-start | bytes 3076
  264.4 30.3 %all-to-all-start.2 = ((bf16[32,64,256]{2,1,0:T(8,128)(2,1)}), bf16[32,64,256]{2,1,0:T(8,128)(2,1)S(1)}, u32[]{:S(2)}, u32[]{:S(2)}) async-start(bf16[32,64,256]{2,1,0:T(8,128)(2,1)} %broadcast_select_fusion), calls=%async_computation.2 | async-start | bytes 2097152 | tf_op jit(solution)/shard_map/all_to_all | solution.py:184
  299.3 3.5 %copy-start.7 = (bf16[13,256]{1,0:T(8,128)(2,1)S(1)}, bf16[13,256]{1,0:T(8,128)(2,1)}, u32[]{:S(2)}) copy-start(bf16[13,256]{1,0:T(8,128)(2,1)} %param.35) | copy-start | bytes 19972
where the time goes:
time: 307 us; the launch traced here: 304 us
  matrix products  117 us (38%)
  local copies, waits for them, and re-layouts  75.3 us (25%)
  waiting for transfers between devices  53.6 us (17%)
  starting transfers between devices  30.3 us (10%)
  other arithmetic  18.9 us (6%)
  loops' own time  8.2 us (3%)
    sub x4, matrix products, one_group(): exp_scores = jnp.exp(scores - row_max)  42.9 us
    dynamic_slice x54, local copies, waits for them, and re-layouts, add_tap(): weights = lax.dynamic_index_in_dim(conv_taps, tap_index, 0, keepdims=False)  38.1 us
    dot_general x54, matrix products, add_tap(): gathered = jnp.dot(picker, window_rows, preferred_element_type=jnp.float32)  34.7 us
    dot_general x4, matrix products, one_group(): jnp.einsum('hqk,hkd->hqd', probs, value_rows, preferred_element_type=jnp....  27.9 us
    all_to_all x1, waiting for transfers between devices, local(): lax.all_to_all(back_feats.reshape(devices, capacity, feat_width), ('row',...  27.5 us
    all_to_all x1, waiting for transfers between devices, local(): lax.all_to_all(send_feats.reshape(devices, capacity, feat_width), ('row',...  26.1 us
    all_to_all x1, starting transfers between devices, local(): lax.all_to_all(send_slots.reshape(devices, capacity), ('row', 'col'), spl...  9.66 us
    scatter x1, local copies, waits for them, and re-layouts, local(): z_feats = jnp.zeros((fine_rows, feat_width), jnp.bfloat16).at[target_slot...  9.53 us
  transfers between devices with their start and end apart: 7, of which 2 were waited for; matrix products, arithmetic and copies ran while one was open for 34% of the time, Pallas kernels for 0%

commit v1 on v0

v1 whole, which is shorter than its diff:
```python
import functools

import jax
import jax.numpy as jnp
from jax import lax
from jax.experimental import pallas as pl
from jax.experimental.pallas import tpu as pltpu
from jax.sharding import PartitionSpec as P

HEADS = 16
PATCH = 1024
REACH = 256
AXES = ("row", "col")
BF = jnp.bfloat16
F32 = jnp.float32
I32 = jnp.int32
VM = pl.BlockSpec(memory_space=pltpu.VMEM)


def dot(a, b):
    return jnp.dot(a, b, preferred_element_type=F32)


def dot_nt(a, b):
    return lax.dot_general(a, b, (((1,), (1,)), ((), ())), preferred_element_type=F32)


def layer_norm(values):
    center = values - jnp.mean(values, axis=-1, keepdims=True)
    spread = jnp.mean(center * center, axis=-1, keepdims=True)
    return center * lax.rsqrt(spread + 1e-05)


def pick(index, rows, cols, dim):
    grid = lax.broadcasted_iota(I32, (rows, cols), dim)
    return jnp.where(grid == index, 1.0, 0.0).astype(BF)


def halo(cells, width, dim):
    count = lax.axis_size(AXES)
    head = lax.slice_in_dim(cells, 0, width, axis=dim)
    tail = lax.slice_in_dim(cells, cells.shape[dim] - width, cells.shape[dim], axis=dim)
    low = lax.ppermute(tail, AXES, [(i, i + 1) for i in range(count - 1)])
    high = lax.ppermute(head, AXES, [(i + 1, i) for i in range(count - 1)])
    return jnp.concatenate([low, cells, high], axis=dim)


def rank_kernel(devices, capacity, z_ref, pos_ref, slot_ref):
    rows = z_ref.shape[1]
    z = z_ref[...]
    dest = z // rows
    slot = z % rows
    onehot = pick(dest, devices, rows, 0)
    before = lax.broadcasted_iota(I32, (rows, rows), 0) < lax.broadcasted_iota(I32, (rows, rows), 1)
    ahead = dot(onehot, jnp.where(before, 1.0, 0.0).astype(BF))
    rank = jnp.sum(ahead * onehot.astype(F32), axis=0, keepdims=True).astype(I32)
    pos = dest * capacity + rank
    pos_ref[...] = pos
    code = slot + 1
    part = lax.broadcasted_iota(I32, (16, rows), 0)
    digits = jnp.where(part == 0, code // 32, jnp.where(part == 1, code % 32, 0))
    digits = digits.astype(F32).astype(BF)
    total = devices * capacity
    step = min(512, total)
    for start in range(0, total, step):
        got = dot_nt(digits, pick(pos - start, step, rows, 0)).astype(I32)
        slot_ref[:, start : start + step] = got[0:1] * 32 + got[1:2] - 1


def conv_kernel(
    coarse_ref, fine_ref, parent_ref, nbr_ref, pos_ref,
    w_parent_ref, w_skip_ref, taps_ref, w_cpe_ref,
    x_ref, send_ref, feat_ref, par_ref,
):
    rows = x_ref.shape[0]
    ext = fine_ref.shape[0]
    coarse = coarse_ref.shape[0]
    par_ref[...] = jax.nn.gelu(layer_norm(dot(coarse_ref[...], w_parent_ref[...]))).astype(BF)
    block = 256

    def join(i, carry):
        at = pl.ds(pl.multiple_of(i * block, block), block)
        chosen = dot(pick(parent_ref[at, :], block, coarse, 1), par_ref[...])
        skip = jax.nn.gelu(layer_norm(dot(fine_ref[at, :], w_skip_ref[...])))
        feat_ref[at, :] = (chosen + skip).astype(BF)
        return carry

    lax.fori_loop(0, ext // block, join, 0)
    window = block + 2 * REACH

    def conv(i, carry):
        base = pl.multiple_of(i * block, block)
        at = pl.ds(base, block)
        cells = feat_ref[pl.ds(base, window), :]
        offsets = nbr_ref[at, :]
        here = lax.broadcasted_iota(I32, offsets.shape, 0) + REACH
        source = jnp.where(offsets != REACH + 1, here + offsets, -1)
        total = jnp.zeros((block, cells.shape[1]), F32)
        for t in range(nbr_ref.shape[1]):
            total = total + dot(pick(source[:, t : t + 1], block, window, 1), cells) * taps_ref[t : t + 1, :]
        out = layer_norm(dot(total.astype(BF), w_cpe_ref[...]))
        center = feat_ref[pl.ds(base + REACH, block), :]
        x_ref[at, :] = (center.astype(F32) + out).astype(BF)
        return carry

    lax.fori_loop(0, rows // block, conv, 0)
    pos = pos_ref[...]

    def pack(i, carry):
        at = pl.ds(pl.multiple_of(i * block, block), block)
        send_ref[at, :] = dot(pick(pos - i * block, block, rows, 0), x_ref[...]).astype(BF)
        return carry

    lax.fori_loop(0, send_ref.shape[0] // block, pack, 0)


def attend_kernel(
    recv_ref, slot_row_ref, slot_col_ref, seg_ref, w_qkv_ref,
    back_ref, q_ref, k_ref, v_ref, fq_ref, fk_ref, acc_ref,
):
    rows, width = acc_ref.shape
    total = recv_ref.shape[0]
    head_dim = width // HEADS
    lanes = 128
    per_group = lanes // head_dim
    block = 256

    def unpack(i, carry):
        at = pl.ds(pl.multiple_of(i * block, block), block)
        z = dot(pick(slot_row_ref[...] - i * block, block, total, 0), recv_ref[...])
        normed = layer_norm(z).astype(BF)
        qkv = dot(normed, w_qkv_ref[...])
        q_ref[at, :] = qkv[:, :width].astype(BF) * jnp.asarray(head_dim**-0.5, BF)
        k_ref[at, :] = qkv[:, width : 2 * width].astype(BF)
        v_ref[at, :] = qkv[:, 2 * width :].astype(BF)
        return carry

    lax.fori_loop(0, rows // block, unpack, 0)
    bits = (PATCH - 1).bit_length()
    lane = lax.broadcasted_iota(I32, (rows, lanes), 1)
    seg = jnp.broadcast_to(seg_ref[...] - seg_ref[0:1, :], (rows, lanes))
    code = ((seg >> (lane // 2)) & 1) ^ (lane & 1)
    used = lane < 2 * bits
    fq_ref[...] = jnp.where(used & (code == 1), 1.0, 0.0).astype(BF)
    fk_ref[...] = jnp.where(used & (code == 0), -1e30, 0.0).astype(BF)
    acc_ref[...] = jnp.zeros_like(acc_ref)
    owner = lane // head_dim

    for g in range(width // lanes):
        cols = slice(g * lanes, (g + 1) * lanes)

        def head(h, carry):
            mine = owner == h
            keys = jnp.where(mine, k_ref[:, cols], jnp.zeros((), BF))
            keys = jnp.concatenate([keys, fk_ref[...]], axis=1)
            values = jnp.where(mine, v_ref[:, cols], jnp.zeros((), BF))
            values = jnp.concatenate([values, jnp.ones((rows, lanes), BF)], axis=1)
            for start in range(0, rows, block):
                at = slice(start, start + block)
                query = jnp.concatenate([q_ref[at, cols], fq_ref[at, :]], axis=1)
                scores = dot_nt(query, keys)
                top = jnp.max(scores, axis=-1, keepdims=True)
                probs = jnp.exp(scores - top).astype(BF)
                out = dot(probs, values)
                acc_ref[at, cols] += out[:, :lanes] / out[:, lanes:]
            return carry

        lax.fori_loop(0, per_group, head, 0)

    q_ref[...] = acc_ref[...].astype(BF)

    def pack(i, carry):
        at = pl.ds(pl.multiple_of(i * block, block), block)
        back_ref[at, :] = dot(pick(slot_col_ref[at, :], block, rows, 1), q_ref[...]).astype(BF)
        return carry

    lax.fori_loop(0, total // block, pack, 0)


def head_kernel(x_ref, back_ref, pos_ref, w_out_ref, w_up_ref, w_down_ref, w_cls_ref, out_ref):
    rows = x_ref.shape[0]
    total = back_ref.shape[0]
    block = 256
    for start in range(0, rows, block):
        at = slice(start, start + block)
        home = dot(pick(pos_ref[at, :], block, total, 1), back_ref[...]).astype(BF)
        o = dot(home, w_out_ref[...]).astype(BF)
        x_two = x_ref[at, :].astype(F32) + o.astype(F32)
        hidden = jax.nn.gelu(dot(layer_norm(x_two).astype(BF), w_up_ref[...])).astype(BF)
        x_three = x_two + dot(hidden, w_down_ref[...])
        out_ref[:, at] = dot_nt(w_cls_ref[...], layer_norm(x_three).astype(BF))


def local(
    coarse_feats,
    fine_feats,
    parent_index,
    nbr_offset,
    z_position,
    segment_id,
    w_parent,
    w_skip,
    conv_taps,
    w_cpe,
    w_qkv,
    w_out,
    w_up,
    w_down,
    w_cls,
):
    fine_rows, width = fine_feats.shape
    coarse_rows = coarse_feats.shape[0]
    devices = lax.axis_size(AXES)
    dev_index = lax.axis_index(AXES)
    capacity = 2 * fine_rows // devices
    total = devices * capacity
    assert fine_rows == PATCH

    pos, slots = pl.pallas_call(
        functools.partial(rank_kernel, devices, capacity),
        out_shape=(
            jax.ShapeDtypeStruct((1, fine_rows), I32),
            jax.ShapeDtypeStruct((1, total), I32),
        ),
        in_specs=[VM],
        out_specs=(VM, VM),
    )(z_position.reshape(1, fine_rows))
    recv_slots = lax.all_to_all(
        slots.reshape(devices, capacity), AXES, split_axis=0, concat_axis=0, tiled=True
    )

    fine_per_coarse = fine_rows // coarse_rows
    margin = coarse_rows // 2 + REACH // fine_per_coarse
    coarse_ext = halo(coarse_feats, margin, 0)
    fine_ext = halo(fine_feats, REACH, 0)
    parent_ext = halo(parent_index, REACH, 0) - (dev_index * coarse_rows - margin)
    ext = fine_rows + 2 * REACH
    x_feats, send = pl.pallas_call(
        conv_kernel,
        out_shape=(
            jax.ShapeDtypeStruct((fine_rows, width), BF),
            jax.ShapeDtypeStruct((total, width), BF),
        ),
        in_specs=[VM] * 9,
        out_specs=(VM, VM),
        scratch_shapes=[
            pltpu.VMEM((ext, width), BF),
            pltpu.VMEM((coarse_ext.shape[0], width), BF),
        ],
    )(
        coarse_ext, fine_ext, parent_ext.reshape(ext, 1), nbr_offset.T, pos,
        w_parent, w_skip, conv_taps, w_cpe,
    )
    recv = lax.all_to_all(
        send.reshape(devices, capacity, width), AXES, split_axis=0, concat_axis=0, tiled=True
    ).reshape(total, width)

    back = pl.pallas_call(
        attend_kernel,
        out_shape=jax.ShapeDtypeStruct((total, width), BF),
        in_specs=[VM] * 5,
        out_specs=VM,
        scratch_shapes=[
            pltpu.VMEM((fine_rows, width), BF),
            pltpu.VMEM((fine_rows, width), BF),
            pltpu.VMEM((fine_rows, width), BF),
            pltpu.VMEM((fine_rows, 128), BF),
            pltpu.VMEM((fine_rows, 128), BF),
            pltpu.VMEM((fine_rows, width), F32),
        ],
    )(
        recv, recv_slots.reshape(1, total), recv_slots.reshape(total, 1),
        segment_id.reshape(fine_rows, 1), w_qkv,
    )
    returned = lax.all_to_all(
        back.reshape(devices, capacity, width), AXES, split_axis=0, concat_axis=0, tiled=True
    ).reshape(total, width)
    return pl.pallas_call(
        head_kernel,
        out_shape=jax.ShapeDtypeStruct((w_cls.shape[0], fine_rows), F32),
        in_specs=[VM] * 7,
        out_specs=VM,
    )(x_feats, returned, pos.reshape(fine_rows, 1), w_out, w_up, w_down, w_cls)


def solution(mesh):
    rows = P(AXES, None)
    flat = P(AXES)
    placed = (rows, rows, flat, P(None, AXES), flat, flat) + (P(),) * 9
    return jax.shard_map(
        local, mesh=mesh, in_specs=placed, out_specs=P(None, AXES), check_vma=False
    )
```

time: 307 us -> 185 us (0.60)
  matrix products: 117 us -> 0 us
  Pallas kernels: 0 us -> 72.8 us
  local copies, waits for them, and re-layouts: 75.3 us -> 12.1 us
  other arithmetic: 18.9 us -> 4.83 us
  starting transfers between devices: 30.3 us -> 40.1 us
  loops' own time: 8.2 us -> 0 us
    dot_general x66 -> x0, matrix products: 74 us -> none  [the longest x54 34.7 us: add_tap(): gathered = jnp.dot(picker, window_rows, preferred_element_type=jnp.float32)]
    pallas_call x0 -> x4, Pallas kernels: none -> 72.8 us  [the longest x1 37.9 us: local(): pl.pallas_call(attend_kernel, out_shape=jax.ShapeDtypeStruct((total, widt...]
    sub x4 -> x0, matrix products: 42.9 us -> none  [one_group(): exp_scores = jnp.exp(scores - row_max)]
    dynamic_slice x116 -> x0, local copies, waits for them, and re-layouts: 40.8 us -> none  [the longest x54 38.1 us: add_tap(): weights = lax.dynamic_index_in_dim(conv_taps, tap_index, 0, keepdims=False)]
    scatter x3 -> x0, local copies, waits for them, and re-layouts: 19.9 us -> none  [the longest x1 9.53 us: local(): z_feats = jnp.zeros((fine_rows, feat_width), jnp.bfloat16).at[target_slot...]
    gather x3 -> x0, local copies, waits for them, and re-layouts: 11.6 us -> none  [the longest x1 7.5 us: local(): back_feats = jnp.take(att_out, back_index, axis=0)]
    another operation x4 -> x0, other arithmetic: 9.15 us -> none
    another operation x4 -> x0, loops' own time: 8.2 us -> none  [the longest x1 6.48 us: local(): conv = lax.map(conv_block, block_starts).reshape(fine_rows, feat_width)]
  transfers between devices with their start and end apart: 7 -> 9, of which waited for: 2 -> 3; matrix products, arithmetic and copies ran while one was open for 34% -> 7% of each run, Pallas kernels for 0% -> 13%
where the time goes in v1:
time: 185 us
  Pallas kernels  72.8 us (39%)
  waiting for transfers between devices  54.7 us (30%)
  starting transfers between devices  40.1 us (22%)
  local copies, waits for them, and re-layouts  12.1 us (7%)
  other arithmetic  4.83 us (3%)
    pallas_call x1, Pallas kernels, local(): pl.pallas_call(attend_kernel, out_shape=jax.ShapeDtypeStruct((total, widt...  37.9 us
    all_to_all x1, waiting for transfers between devices, local(): lax.all_to_all(back.reshape(devices, capacity, width), AXES, split_axis=0...  26.4 us
    all_to_all x1, waiting for transfers between devices, local(): lax.all_to_all(send.reshape(devices, capacity, width), AXES, split_axis=0...  22.9 us
    pallas_call x1, Pallas kernels, local(): pl.pallas_call(conv_kernel, out_shape=(jax.ShapeDtypeStruct((fine_rows, w...  22 us
    ppermute x3, starting transfers between devices, halo(): low = lax.ppermute(tail, AXES, [(i, i + 1) for i in range(count - 1)])  14.4 us
    all_to_all x1, starting transfers between devices, local(): lax.all_to_all(slots.reshape(devices, capacity), AXES, split_axis=0, conc...  10.5 us
    pallas_call x1, Pallas kernels, local(): pl.pallas_call(head_kernel, out_shape=jax.ShapeDtypeStruct((w_cls.shape[0...  10.1 us
    all_to_all x1, starting transfers between devices, local(): lax.all_to_all(send.reshape(devices, capacity, width), AXES, split_axis=0...  8.57 us
  transfers between devices with their start and end apart: 9, of which 3 were waited for; matrix products, arithmetic and copies ran while one was open for 7% of the time, Pallas kernels for 13%

profile of v1, /device:TPU:0, one launch (start us, length us, event | category | flops | bytes accessed | tf_op | source)
XLA Modules:
  0.0 184.7 jit_solution(5445147555858686030)
XLA Ops:
  0.8 4.9 %collective-permute-start.4 = (s32[256]{0:T(256)S(1)}, s32[256]{0:T(256)S(1)}, u32[]{:S(2)}, u32[]{:S(2)}) collective-permute-start(s32[256]{0:T(256)S(1)} %get-tuple-element.17), channel_id=1, source_target_pairs={{0,1},{1,2},{2,3},{3,4},{4,5},{5,6},{6,7},{7,8},{8,9},{9,10},{10,1... | collective-permute-start | bytes 3080 | tf_op jit(solution)/shard_map/ppermute | solution.py:43
  5.7 1.3 collective-permute-start.5
  7.0 1.0 fusion
  8.0 4.6 %collective-permute-start.2 = (bf16[256,256]{1,0:T(8,128)(2,1)S(1)}, bf16[256,256]{1,0:T(8,128)(2,1)S(1)}, u32[]{:S(2)}, u32[]{:S(2)}) collective-permute-start(bf16[256,256]{1,0:T(8,128)(2,1)S(1)} %get-tuple-element.13), channel_id=1, source_target_pairs={{0,1},{1,2},{2,3},{3,4},{4,5},{5,6},{6,7},{7,8},{8,9},{9,10},{10,1... | collective-permute-start | bytes 393224 | tf_op jit(solution)/shard_map/ppermute | solution.py:43
  12.6 1.3 collective-permute-start.3
  13.9 1.1 fusion.1
  14.9 5.0 %collective-permute-start = (bf16[192,512]{1,0:T(8,128)(2,1)S(1)}, bf16[192,512]{1,0:T(8,128)(2,1)S(1)}, u32[]{:S(2)}, u32[]{:S(2)}) collective-permute-start(bf16[192,512]{1,0:T(8,128)(2,1)S(1)} %get-tuple-element.15), channel_id=1, source_target_pairs={{0,1},{1,2},{2,3},{3,4},{4,5},{5,6},{6,7},{7,8},{8,9},{9,10},{10,1... | collective-permute-start | bytes 589832 | tf_op jit(solution)/shard_map/ppermute | solution.py:43
  19.9 2.8 %shard_map.145 = (s32[1,1024]{1,0:T(1,128)}, s32[1,2048]{1,0:T(1,128)}) custom-call(s32[1,1024]{1,0:T(1,128)} %bitcast.22), custom_call_target="tpu_custom_call" | custom-call | tf_op jit(solution)/shard_map/pallas_call | solution.py:219
  23.3 1.4 reduce.8
  25.3 10.5 %all-to-all-start.1 = ((s32[32,1,64]{2,1,0:T(1,128)}), s32[32,1,64]{2,1,0:T(1,128)S(1)}, u32[]{:S(2)}, u32[]{:S(2)}) async-start(s32[32,1,64]{2,1,0:T(1,128)} %bitcast.7), calls=%async_computation.1 | async-start | bytes 32768 | tf_op jit(solution)/shard_map/all_to_all | solution.py:228
  35.8 1.0 copy.32
  36.8 1.3 collective-permute-start.1
  40.4 5.4 %collective-permute-done.1 = bf16[192,512]{1,0:T(8,128)(2,1)S(1)} collective-permute-done((bf16[192,512]{1,0:T(8,128)(2,1)S(1)}, bf16[192,512]{1,0:T(8,128)(2,1)S(1)}, u32[]{:S(2)}, u32[]{:S(2)}) %collective-permute-start.1) | collective-permute-done | bytes 196640 | tf_op jit(solution)/shard_map/ppermute | solution.py:44
  46.7 22.0 %shard_map.146 = (bf16[1024,256]{1,0:T(8,128)(2,1)}, bf16[2048,256]{1,0:T(8,128)(2,1)}) custom-call(bf16[640,512]{1,0:T(8,128)(2,1)} %pad_maximum_fusion.1.coarse_ref, bf16[1536,256]{1,0:T(8,128)(2,1)} %pad_maximum_fusion.fine_ref, s32[1536,1]{1,0:T(8,128)} %broadcast_subtract_fusion.parent_ref, s32[1024,27]{1,0:T(8,128)} %bitcast.16, ...), custom_call_target="tpu_custom_call" | custom-call | tf_op jit(solution)/shard_map/pallas_call | solution.py:238
  68.7 8.6 %all-to-all-start = ((bf16[32,64,256]{2,1,0:T(8,128)(2,1)}), bf16[32,64,256]{2,1,0:T(8,128)(2,1)S(1)}, u32[]{:S(2)}, u32[]{:S(2)}) async-start(bf16[32,64,256]{2,1,0:T(8,128)(2,1)} %bitcast.17), calls=%async_computation | async-start | bytes 2097152 | tf_op jit(solution)/shard_map/all_to_all | solution.py:254
  77.3 1.0 copy.35.seg_ref
  79.7 2.0 %reshape.85.slot_col_ref = s32[2048,1]{1,0:T(8,128)} reshape(s32[32,64]{1,0:T(8,128)S(1)} %bitcast.18) | data formatting | bytes 16384 | tf_op jit(solution)/shard_map/reshape | solution.py:272
  81.7 22.9 %all-to-all-done = bf16[32,64,256]{2,1,0:T(8,128)(2,1)S(1)} async-done(((bf16[32,64,256]{2,1,0:T(8,128)(2,1)}), bf16[32,64,256]{2,1,0:T(8,128)(2,1)S(1)}, u32[]{:S(2)}, u32[]{:S(2)}) %all-to-all-start) | async-done | bytes 1048608 | tf_op jit(solution)/shard_map/all_to_all | solution.py:254
  105.5 37.9 %shard_map.147 = bf16[2048,256]{1,0:T(8,128)(2,1)} custom-call(bf16[2048,256]{1,0:T(8,128)(2,1)} %bitcast.14, s32[1,2048]{1,0:T(1,128)} %reshape.79.slot_row_ref, s32[2048,1]{1,0:T(8,128)} %reshape.85.slot_col_ref, s32[1024,1]{1,0:T(8,128)} %copy.35.seg_ref, bf16[256,768]{1,0:T(8,128)(2,1)} %w_qkv_ref.1), custom_call_target="tpu_custom_call" | custom-call | tf_op jit(solution)/shard_map/pallas_call | solution.py:258
  143.4 2.8 %all-to-all-start.2 = ((bf16[32,64,256]{2,1,0:T(8,128)(2,1)}), bf16[32,64,256]{2,1,0:T(8,128)(2,1)S(1)}, u32[]{:S(2)}, u32[]{:S(2)}) async-start(bf16[32,64,256]{2,1,0:T(8,128)(2,1)} %bitcast.15), calls=%async_computation.2 | async-start | bytes 2097152 | tf_op jit(solution)/shard_map/all_to_all | solution.py:275
  146.2 1.0 copy.36.pos_ref
  147.3 26.4 %all-to-all-done.2 = bf16[32,64,256]{2,1,0:T(8,128)(2,1)S(1)} async-done(((bf16[32,64,256]{2,1,0:T(8,128)(2,1)}), bf16[32,64,256]{2,1,0:T(8,128)(2,1)S(1)}, u32[]{:S(2)}, u32[]{:S(2)}) %all-to-all-start.2) | async-done | bytes 1048608 | tf_op jit(solution)/shard_map/all_to_all | solution.py:275
  173.7 1.0 copy-done
  174.7 10.1 %shard_map.148 = f32[13,1024]{1,0:T(8,128)} custom-call(bf16[1024,256]{1,0:T(8,128)(2,1)} %get-tuple-element.10.x_ref, bf16[2048,256]{1,0:T(8,128)(2,1)} %bitcast.13, s32[1024,1]{1,0:T(8,128)} %copy.36.pos_ref, bf16[256,256]{1,0:T(8,128)(2,1)} %w_out_ref.1, bf16[256,1024]{1,0:T(8,128)(2,1)} %w_up_ref.1, bf16[1024,256]{1,0:T(8,128)(2,1)} %w_down_ref.1, ...), custom_call_target="tpu_custom_call" | custom-call | tf_op jit(solution)/shard_map/pallas_call | solution.py:278
  (31 shorter events, 7.5 us)
Async XLA Ops:
  0.0 38.1 %copy-start.6 = (s32[1024]{0:T(1024)S(1)}, s32[1024]{0:T(1024)}, u32[]{:S(2)}) copy-start(s32[1024]{0:T(1024)} %param.17) | copy-start | bytes 12292
  0.0 35.8 %copy-start.4 = (s32[27,1024]{1,0:T(8,128)S(1)}, s32[27,1024]{1,0:T(8,128)}, u32[]{:S(2)}) copy-start(s32[27,1024]{1,0:T(8,128)} %param.18) | copy-start | bytes 331780
  0.8 36.0 %collective-permute-start.4 = (s32[256]{0:T(256)S(1)}, s32[256]{0:T(256)S(1)}, u32[]{:S(2)}, u32[]{:S(2)}) collective-permute-start(s32[256]{0:T(256)S(1)} %get-tuple-element.17), channel_id=1, source_target_pairs={{0,1},{1,2},{2,3},{3,4},{4,5},{5,6},{6,7},{7,8},{8,9},{9,10},{10,1... | collective-permute-start | bytes 3080 | tf_op jit(solution)/shard_map/ppermute | solution.py:43
  5.7 32.4 %collective-permute-start.5 = (s32[256]{0:T(256)S(1)}, s32[256]{0:T(256)S(1)}, u32[]{:S(2)}, u32[]{:S(2)}) collective-permute-start(s32[256]{0:T(256)S(1)} %get-tuple-element.18), channel_id=1, source_target_pairs={{1,0},{2,1},{3,2},{4,3},{5,4},{6,5},{7,6},{8,7},{9,8},{10,9},{11,1... | collective-permute-start | bytes 3080 | tf_op jit(solution)/shard_map/ppermute | solution.py:44
  8.0 31.4 %collective-permute-start.2 = (bf16[256,256]{1,0:T(8,128)(2,1)S(1)}, bf16[256,256]{1,0:T(8,128)(2,1)S(1)}, u32[]{:S(2)}, u32[]{:S(2)}) collective-permute-start(bf16[256,256]{1,0:T(8,128)(2,1)S(1)} %get-tuple-element.13), channel_id=1, source_target_pairs={{0,1},{1,2},{2,3},{3,4},{4,5},{5,6},{6,7},{7,8},{8,9},{9,10},{10,1... | collective-permute-start | bytes 393224 | tf_op jit(solution)/shard_map/ppermute | solution.py:43
  12.6 26.9 %collective-permute-start.3 = (bf16[256,256]{1,0:T(8,128)(2,1)S(1)}, bf16[256,256]{1,0:T(8,128)(2,1)S(1)}, u32[]{:S(2)}, u32[]{:S(2)}) collective-permute-start(bf16[256,256]{1,0:T(8,128)(2,1)S(1)} %get-tuple-element.14), channel_id=1, source_target_pairs={{1,0},{2,1},{3,2},{4,3},{5,4},{6,5},{7,6},{8,7},{9,8},{10,9},{11,1... | collective-permute-start | bytes 393224 | tf_op jit(solution)/shard_map/ppermute | solution.py:44
  14.9 25.5 %collective-permute-start = (bf16[192,512]{1,0:T(8,128)(2,1)S(1)}, bf16[192,512]{1,0:T(8,128)(2,1)S(1)}, u32[]{:S(2)}, u32[]{:S(2)}) collective-permute-start(bf16[192,512]{1,0:T(8,128)(2,1)S(1)} %get-tuple-element.15), channel_id=1, source_target_pairs={{0,1},{1,2},{2,3},{3,4},{4,5},{5,6},{6,7},{7,8},{8,9},{9,10},{10,1... | collective-permute-start | bytes 589832 | tf_op jit(solution)/shard_map/ppermute | solution.py:43
  25.3 43.4 %all-to-all-start.1 = ((s32[32,1,64]{2,1,0:T(1,128)}), s32[32,1,64]{2,1,0:T(1,128)S(1)}, u32[]{:S(2)}, u32[]{:S(2)}) async-start(s32[32,1,64]{2,1,0:T(1,128)} %bitcast.7), calls=%async_computation.1 | async-start | bytes 32768 | tf_op jit(solution)/shard_map/all_to_all | solution.py:228
  36.8 9.0 %collective-permute-start.1 = (bf16[192,512]{1,0:T(8,128)(2,1)S(1)}, bf16[192,512]{1,0:T(8,128)(2,1)S(1)}, u32[]{:S(2)}, u32[]{:S(2)}) collective-permute-start(bf16[192,512]{1,0:T(8,128)(2,1)S(1)} %get-tuple-element.16), channel_id=1, source_target_pairs={{1,0},{2,1},{3,2},{4,3},{5,4},{6,5},{7,6},{8,7},{9,8},{10,9},{11,1... | collective-permute-start | bytes 589832 | tf_op jit(solution)/shard_map/ppermute | solution.py:44
  38.2 1.3 copy-start.3
  39.4 6.4 %copy-start.2 = (bf16[256,512]{1,0:T(8,128)(2,1)S(1)}, bf16[256,512]{1,0:T(8,128)(2,1)}, u32[]{:S(2)}) copy-start(bf16[256,512]{1,0:T(8,128)(2,1)} %param.15) | copy-start | bytes 786436
  68.7 8.6 %copy-start.7 = (s32[1024]{0:T(1024)S(1)}, s32[1024]{0:T(1024)}, u32[]{:S(2)}) copy-start(s32[1024]{0:T(1024)} %param.20) | copy-start | bytes 12292
  68.7 35.9 %all-to-all-start = ((bf16[32,64,256]{2,1,0:T(8,128)(2,1)}), bf16[32,64,256]{2,1,0:T(8,128)(2,1)S(1)}, u32[]{:S(2)}, u32[]{:S(2)}) async-start(bf16[32,64,256]{2,1,0:T(8,128)(2,1)} %bitcast.17), calls=%async_computation | async-start | bytes 2097152 | tf_op jit(solution)/shard_map/all_to_all | solution.py:254
  104.6 1.0 copy-start.1
  143.4 2.8 %copy-start.5 = (s32[1,1024]{1,0:T(1,128)S(1)}, s32[1,1024]{1,0:T(1,128)}, u32[]{:S(2)}) copy-start(s32[1,1024]{1,0:T(1,128)} %get-tuple-element.9.pos_ref) | copy-start | bytes 12292
  143.4 30.3 %all-to-all-start.2 = ((bf16[32,64,256]{2,1,0:T(8,128)(2,1)}), bf16[32,64,256]{2,1,0:T(8,128)(2,1)S(1)}, u32[]{:S(2)}, u32[]{:S(2)}) async-start(bf16[32,64,256]{2,1,0:T(8,128)(2,1)} %bitcast.15), calls=%async_computation.2 | async-start | bytes 2097152 | tf_op jit(solution)/shard_map/all_to_all | solution.py:275
  173.7 1.0 copy-start

commit v2 on v1

--- a/solution.py
+++ b/solution.py
@@ -36,23 +36,119 @@
     return jnp.where(grid == index, 1.0, 0.0).astype(BF)
 
 
-def halo(cells, width, dim):
-    count = lax.axis_size(AXES)
-    head = lax.slice_in_dim(cells, 0, width, axis=dim)
-    tail = lax.slice_in_dim(cells, cells.shape[dim] - width, cells.shape[dim], axis=dim)
-    low = lax.ppermute(tail, AXES, [(i, i + 1) for i in range(count - 1)])
-    high = lax.ppermute(head, AXES, [(i + 1, i) for i in range(count - 1)])
-    return jnp.concatenate([low, cells, high], axis=dim)
-
-
-def rank_kernel(devices, capacity, z_ref, pos_ref, slot_ref):
+def column(row):
+    return jnp.broadcast_to(row, (128, row.shape[1])).T[:, :1]
+
+
+def place(device):
+    inner = lax.axis_size("col")
+    return (device // inner, device % inner)
+
+
+def greet(me, devices):
+    barrier = pltpu.get_barrier_semaphore()
+
+    def signal(k, carry):
+        pl.semaphore_signal(
+            barrier, inc=1, device_id=place((me + k) % devices),
+            device_id_type=pl.DeviceIdType.MESH,
+        )
+        return carry
+
+    lax.fori_loop(1, devices, signal, 0)
+    pl.semaphore_wait(barrier, devices - 1)
+
+
+def ship(src, dst, send_sem, recv_sem, device):
+    return pltpu.make_async_remote_copy(
+        src_ref=src, dst_ref=dst, send_sem=send_sem, recv_sem=recv_sem,
+        device_id=place(device), device_id_type=pl.DeviceIdType.MESH,
+    )
+
+
+def spread(src_ref, dst_ref, send_sems, recv_sems, me, devices):
+    def start(k, carry):
+        peer = (me + k) % devices
+        ship(
+            src_ref.at[peer], dst_ref.at[me], send_sems.at[peer], recv_sems.at[me], peer
+        ).start()
+        return carry
+
+    lax.fori_loop(1, devices, start, 0)
+
+
+def gather_in(src_ref, dst_ref, send_sems, recv_sems, me, devices):
+    def finish(k, carry):
+        peer = (me + k) % devices
+        ship(
+            src_ref.at[peer], dst_ref.at[peer], send_sems.at[peer], recv_sems.at[peer], peer
+        ).wait()
+        return carry
+
+    lax.fori_loop(1, devices, finish, 0)
+
+
+def trade_kernel(devices, src_ref, dst_ref, send_sems, recv_sems):
+    me = lax.axis_index(AXES)
+    greet(me, devices)
+    spread(src_ref, dst_ref, send_sems, recv_sems, me, devices)
+    dst_ref[me] = src_ref[me]
+    gather_in(src_ref, dst_ref, send_sems, recv_sems, me, devices)
+
+
+def trade(cells, collective_id):
+    devices = cells.shape[0]
+    return pl.pallas_call(
+        functools.partial(trade_kernel, devices),
+        out_shape=jax.ShapeDtypeStruct(cells.shape, cells.dtype),
+        in_specs=[VM],
+        out_specs=VM,
+        scratch_shapes=[
+            pltpu.SemaphoreType.DMA((devices,)),
+            pltpu.SemaphoreType.DMA((devices,)),
+        ],
+        compiler_params=pltpu.CompilerParams(
+            collective_id=collective_id, has_side_effects=True
+        ),
+    )(cells)
+
+
+def open_kernel(
+    devices, capacity, z_ref, coarse_ref, fine_ref, parent_ref,
+    pos_ref, got_ref, coarse_out, fine_out, parent_out,
+    slot_ref, take_ref, send_sems, recv_sems, send_side, recv_side,
+):
+    me = lax.axis_index(AXES)
+    greet(me, devices)
+    after, before = (me + 1) % devices, (me + devices - 1) % devices
+    moves = []
+    for j, (src, dst, dim) in enumerate(
+        ((coarse_ref, coarse_out, 0), (fine_ref, fine_out, 0), (parent_ref, parent_out, 1))
+    ):
+        size = src.shape[dim]
+        width = (dst.shape[dim] - size) // 2
+
+        def cut(ref, at, count, dim=dim):
+            return ref.at[pl.ds(at, count), :] if dim == 0 else ref.at[:, pl.ds(at, count)]
+
+        moves.append(ship(
+            cut(src, size - width, width), cut(dst, 0, width),
+            send_side.at[2 * j], recv_side.at[2 * j], after,
+        ))
+        moves.append(ship(
+            cut(src, 0, width), cut(dst, size + width, width),
+            send_side.at[2 * j + 1], recv_side.at[2 * j + 1], before,
+        ))
+    for move in moves:
+        move.start()
+
     rows = z_ref.shape[1]
     z = z_ref[...]
     dest = z // rows
     slot = z % rows
     onehot = pick(dest, devices, rows, 0)
-    before = lax.broadcasted_iota(I32, (rows, rows), 0) < lax.broadcasted_iota(I32, (rows, rows), 1)
-    ahead = dot(onehot, jnp.where(before, 1.0, 0.0).astype(BF))
+    earlier = lax.broadcasted_iota(I32, (rows, rows), 0) < lax.broadcasted_iota(I32, (rows, rows), 1)
+    ahead = dot(onehot, jnp.where(earlier, 1.0, 0.0).astype(BF))
     rank = jnp.sum(ahead * onehot.astype(F32), axis=0, keepdims=True).astype(I32)
     pos = dest * capacity + rank
     pos_ref[...] = pos
@@ -64,11 +160,30 @@
     step = min(512, total)
     for start in range(0, total, step):
         got = dot_nt(digits, pick(pos - start, step, rows, 0)).astype(I32)
-        slot_ref[:, start : start + step] = got[0:1] * 32 + got[1:2] - 1
+        got = got[0:1] * 32 + got[1:2] - 1
+        for d in range(step // capacity):
+            slot_ref[start // capacity + d] = got[:, d * capacity : (d + 1) * capacity]
+
+    spread(slot_ref, take_ref, send_sems, recv_sems, me, devices)
+    take_ref[me] = slot_ref[me]
+    for src, dst, dim in (
+        (coarse_ref, coarse_out, 0), (fine_ref, fine_out, 0), (parent_ref, parent_out, 1)
+    ):
+        size = src.shape[dim]
+        width = (dst.shape[dim] - size) // 2
+        if dim == 0:
+            dst[width : width + size, :] = src[...]
+        else:
+            dst[:, width : width + size] = src[...]
+    for move in moves:
+        move.wait()
+    gather_in(slot_ref, take_ref, send_sems, recv_sems, me, devices)
+    for d in range(devices):
+        got_ref[:, d * capacity : (d + 1) * capacity] = take_ref[d]
 
 
 def conv_kernel(
-    coarse_ref, fine_ref, parent_ref, nbr_ref, pos_ref,
+    margin, coarse_ref, fine_ref, parent_ref, nbr_ref, pos_ref,
     w_parent_ref, w_skip_ref, taps_ref, w_cpe_ref,
     x_ref, send_ref, feat_ref, par_ref,
 ):
@@ -77,10 +192,12 @@
     coarse = coarse_ref.shape[0]
     par_ref[...] = jax.nn.gelu(layer_norm(dot(coarse_ref[...], w_parent_ref[...]))).astype(BF)
     block = 256
+    base_row = lax.axis_index(AXES) * (coarse - 2 * margin) - margin
 
     def join(i, carry):
         at = pl.ds(pl.multiple_of(i * block, block), block)
-        chosen = dot(pick(parent_ref[at, :], block, coarse, 1), par_ref[...])
+        rows_at = column(parent_ref[:, at] - base_row)
+        chosen = dot(pick(rows_at, block, coarse, 1), par_ref[...])
         skip = jax.nn.gelu(layer_norm(dot(fine_ref[at, :], w_skip_ref[...])))
         feat_ref[at, :] = (chosen + skip).astype(BF)
         return carry
@@ -92,11 +209,11 @@
         base = pl.multiple_of(i * block, block)
         at = pl.ds(base, block)
         cells = feat_ref[pl.ds(base, window), :]
-        offsets = nbr_ref[at, :]
+        offsets = nbr_ref[:, at].T
         here = lax.broadcasted_iota(I32, offsets.shape, 0) + REACH
         source = jnp.where(offsets != REACH + 1, here + offsets, -1)
         total = jnp.zeros((block, cells.shape[1]), F32)
-        for t in range(nbr_ref.shape[1]):
+        for t in range(nbr_ref.shape[0]):
             total = total + dot(pick(source[:, t : t + 1], block, window, 1), cells) * taps_ref[t : t + 1, :]
         out = layer_norm(dot(total.astype(BF), w_cpe_ref[...]))
         center = feat_ref[pl.ds(base + REACH, block), :]
@@ -115,7 +232,7 @@
 
 
 def attend_kernel(
-    recv_ref, slot_row_ref, slot_col_ref, seg_ref, w_qkv_ref,
+    recv_ref, slot_row_ref, seg_ref, w_qkv_ref,
     back_ref, q_ref, k_ref, v_ref, fq_ref, fk_ref, acc_ref,
 ):
     rows, width = acc_ref.shape
@@ -138,7 +255,7 @@
     lax.fori_loop(0, rows // block, unpack, 0)
     bits = (PATCH - 1).bit_length()
     lane = lax.broadcasted_iota(I32, (rows, lanes), 1)
-    seg = jnp.broadcast_to(seg_ref[...] - seg_ref[0:1, :], (rows, lanes))
+    seg = jnp.broadcast_to(seg_ref[...] - seg_ref[:, 0:1], (lanes, rows)).T
     code = ((seg >> (lane // 2)) & 1) ^ (lane & 1)
     used = lane < 2 * bits
     fq_ref[...] = jnp.where(used & (code == 1), 1.0, 0.0).astype(BF)
@@ -171,7 +288,7 @@
 
     def pack(i, carry):
         at = pl.ds(pl.multiple_of(i * block, block), block)
-        back_ref[at, :] = dot(pick(slot_col_ref[at, :], block, rows, 1), q_ref[...]).astype(BF)
+        back_ref[at, :] = dot(pick(column(slot_row_ref[:, at]), block, rows, 1), q_ref[...]).astype(BF)
         return carry
 
     lax.fori_loop(0, total // block, pack, 0)
@@ -183,7 +300,7 @@
     block = 256
     for start in range(0, rows, block):
         at = slice(start, start + block)
-        home = dot(pick(pos_ref[at, :], block, total, 1), back_ref[...]).astype(BF)
+        home = dot(pick(column(pos_ref[:, at]), block, total, 1), back_ref[...]).astype(BF)
         o = dot(home, w_out_ref[...]).astype(BF)
         x_two = x_ref[at, :].astype(F32) + o.astype(F32)
         hidden = jax.nn.gelu(dot(layer_norm(x_two).astype(BF), w_up_ref[...])).astype(BF)
@@ -211,32 +328,40 @@
     fine_rows, width = fine_feats.shape
     coarse_rows = coarse_feats.shape[0]
     devices = lax.axis_size(AXES)
-    dev_index = lax.axis_index(AXES)
     capacity = 2 * fine_rows // devices
     total = devices * capacity
     assert fine_rows == PATCH
 
-    pos, slots = pl.pallas_call(
-        functools.partial(rank_kernel, devices, capacity),
+    fine_per_coarse = fine_rows // coarse_rows
+    margin = coarse_rows // 2 + REACH // fine_per_coarse
+    ext = fine_rows + 2 * REACH
+    coarse_ext_rows = coarse_rows + 2 * margin
+    pos, slots, coarse_ext, fine_ext, parent_ext = pl.pallas_call(
+        functools.partial(open_kernel, devices, capacity),
         out_shape=(
             jax.ShapeDtypeStruct((1, fine_rows), I32),
             jax.ShapeDtypeStruct((1, total), I32),
+            jax.ShapeDtypeStruct((coarse_ext_rows, coarse_feats.shape[1]), BF),
+            jax.ShapeDtypeStruct((ext, width), BF),
+            jax.ShapeDtypeStruct((1, ext), I32),
         ),
-        in_specs=[VM],
-        out_specs=(VM, VM),
-    )(z_position.reshape(1, fine_rows))
-    recv_slots = lax.all_to_all(
-        slots.reshape(devices, capacity), AXES, split_axis=0, concat_axis=0, tiled=True
+        in_specs=[VM] * 4,
+        out_specs=(VM,) * 5,
+        scratch_shapes=[
+            pltpu.VMEM((devices, 1, capacity), I32),
+            pltpu.VMEM((devices, 1, capacity), I32),
+            pltpu.SemaphoreType.DMA((devices,)),
+            pltpu.SemaphoreType.DMA((devices,)),
+            pltpu.SemaphoreType.DMA((6,)),
+            pltpu.SemaphoreType.DMA((6,)),
+        ],
+        compiler_params=pltpu.CompilerParams(collective_id=0, has_side_effects=True),
+    )(
+        z_position.reshape(1, fine_rows), coarse_feats, fine_feats,
+        parent_index.reshape(1, fine_rows),
     )
-
-    fine_per_coarse = fine_rows // coarse_rows
-    margin = coarse_rows // 2 + REACH // fine_per_coarse
-    coarse_ext = halo(coarse_feats, margin, 0)
-    fine_ext = halo(fine_feats, REACH, 0)
-    parent_ext = halo(parent_index, REACH, 0) - (dev_index * coarse_rows - margin)
-    ext = fine_rows + 2 * REACH
     x_feats, send = pl.pallas_call(
-        conv_kernel,
+        functools.partial(conv_kernel, margin),
         out_shape=(
             jax.ShapeDtypeStruct((fine_rows, width), BF),
             jax.ShapeDtypeStruct((total, width), BF),
@@ -245,20 +370,18 @@
         out_specs=(VM, VM),
         scratch_shapes=[
             pltpu.VMEM((ext, width), BF),
-            pltpu.VMEM((coarse_ext.shape[0], width), BF),
+            pltpu.VMEM((coarse_ext_rows, width), BF),
         ],
     )(
-        coarse_ext, fine_ext, parent_ext.reshape(ext, 1), nbr_offset.T, pos,
+        coarse_ext, fine_ext, parent_ext, nbr_offset, pos,
         w_parent, w_skip, conv_taps, w_cpe,
     )
-    recv = lax.all_to_all(
-        send.reshape(devices, capacity, width), AXES, split_axis=0, concat_axis=0, tiled=True
-    ).reshape(total, width)
+    recv = trade(send.reshape(devices, capacity, width), 1).reshape(total, width)
 
     back = pl.pallas_call(
         attend_kernel,
         out_shape=jax.ShapeDtypeStruct((total, width), BF),
-        in_specs=[VM] * 5,
+        in_specs=[VM] * 4,
         out_specs=VM,
         scratch_shapes=[
             pltpu.VMEM((fine_rows, width), BF),
@@ -268,19 +391,14 @@
             pltpu.VMEM((fine_rows, 128), BF),
             pltpu.VMEM((fine_rows, width), F32),
         ],
-    )(
-        recv, recv_slots.reshape(1, total), recv_slots.reshape(total, 1),
-        segment_id.reshape(fine_rows, 1), w_qkv,
-    )
-    returned = lax.all_to_all(
-        back.reshape(devices, capacity, width), AXES, split_axis=0, concat_axis=0, tiled=True
-    ).reshape(total, width)
+    )(recv, slots, segment_id.reshape(1, fine_rows), w_qkv)
+    returned = trade(back.reshape(devices, capacity, width), 2).reshape(total, width)
     return pl.pallas_call(
         head_kernel,
         out_shape=jax.ShapeDtypeStruct((w_cls.shape[0], fine_rows), F32),
         in_specs=[VM] * 7,
         out_specs=VM,
-    )(x_feats, returned, pos.reshape(fine_rows, 1), w_out, w_up, w_down, w_cls)
+    )(x_feats, returned, pos, w_out, w_up, w_down, w_cls)
 
 
 def solution(mesh):

time: 185 us -> 158 us (0.85)
  Pallas kernels: 72.8 us -> 157 us
  waiting for transfers between devices: 54.7 us -> 0 us
  starting transfers between devices: 40.1 us -> 0 us
  local copies, waits for them, and re-layouts: 12.1 us -> 0 us
  other arithmetic: 4.83 us -> 0 us
    pallas_call x2 -> x4, Pallas kernels: 24.9 us -> 109 us  [the longest x2 59.6 us: trade(): pl.pallas_call(functools.partial(trade_kernel, devices), out_shape=jax.Sh...]
    all_to_all x3 -> x0, waiting for transfers between devices: 49.3 us -> none  [the longest x1 26.4 us: local(): lax.all_to_all(back.reshape(devices, capacity, width), AXES, split_axis=0...]
    all_to_all x3 -> x0, starting transfers between devices: 21.8 us -> none  [the longest x1 10.5 us: local(): lax.all_to_all(slots.reshape(devices, capacity), AXES, split_axis=0, conc...]
    ppermute x6 -> x0, starting transfers between devices: 18.3 us -> none  [the longest x3 14.4 us: halo(): low = lax.ppermute(tail, AXES, [(i, i + 1) for i in range(count - 1)])]
    ppermute x6 -> x0, waiting for transfers between devices: 5.39 us -> none  [the longest x3 5.39 us: halo(): high = lax.ppermute(head, AXES, [(i + 1, i) for i in range(count - 1)])]
    reshape x4 -> x0, local copies, waits for them, and re-layouts: 4.74 us -> none  [the longest x1 2 us: local(): recv_slots.reshape(total, 1)]
    unnamed x17 -> x0, local copies, waits for them, and re-layouts: 2.98 us -> none
    slice x3 -> x0, local copies, waits for them, and re-layouts: 2.87 us -> none  [halo(): lax.slice_in_dim(cells, cells.shape[dim] - width, cells.shape[dim], axis=...]
  transfers between devices with their start and end apart: 9 -> 0, of which waited for: 3 -> 0; matrix products, arithmetic and copies ran while one was open for 7% -> 0% of each run, Pallas kernels for 13% -> 0%
where the time goes in v2:
time: 158 us; the launch traced here: 157 us
  Pallas kernels  157 us (99%)
    pallas_call x2, Pallas kernels, trade(): pl.pallas_call(functools.partial(trade_kernel, devices), out_shape=jax.Sh...  59.6 us
    pallas_call x1, Pallas kernels, local(): pl.pallas_call(attend_kernel, out_shape=jax.ShapeDtypeStruct((total, widt...  38.5 us
    pallas_call x1, Pallas kernels, local(): pl.pallas_call(functools.partial(open_kernel, devices, capacity), out_sha...  26.2 us
    pallas_call x1, Pallas kernels, local(): pl.pallas_call(functools.partial(conv_kernel, margin), out_shape=(jax.Sha...  22.9 us
    pallas_call x1, Pallas kernels, local(): pl.pallas_call(head_kernel, out_shape=jax.ShapeDtypeStruct((w_cls.shape[0...  10.4 us

profile of v2, /device:TPU:0, one launch (start us, length us, event | category | flops | bytes accessed | tf_op | source)
XLA Modules:
  0.0 157.5 jit_solution(4336071540921102294)
XLA Ops:
  0.0 26.2 %shard_map.145 = (s32[1,1024]{1,0:T(1,128)}, s32[1,2048]{1,0:T(1,128)}, bf16[640,512]{1,0:T(8,128)(2,1)}, bf16[1536,256]{1,0:T(8,128)(2,1)}, s32[1,1536]{1,0:T(1,128)}) custom-call(s32[1,1024]{1,0:T(1,128)} %bitcast.11, bf16[256,512]{1,0:T(8,128)(2,1)} %coarse_ref.1, bf16[1024,256]{1,0:T(8,128)(2,1)} %fine_ref.1, s32[1,1024]{1,0:T(1,128)} %bitcast.12), custom_call_target="tpu_custom_call" | custom-call | tf_op jit(solution)/shard_map/pallas_call | solution.py:339
  26.2 22.9 %shard_map.146 = (bf16[1024,256]{1,0:T(8,128)(2,1)}, bf16[2048,256]{1,0:T(8,128)(2,1)}) custom-call(bf16[640,512]{1,0:T(8,128)(2,1)} %get-tuple-element.12.coarse_ref, bf16[1536,256]{1,0:T(8,128)(2,1)} %get-tuple-element.13.fine_ref, s32[1,1536]{1,0:T(1,128)} %get-tuple-element.14.parent_ref, s32[27,1024]{1,0:T(8,128)} %nbr_ref.1, ...), custom_call_target="tpu_custom_call" | custom-call | tf_op jit(solution)/shard_map/pallas_call | solution.py:363
  49.1 29.6 %shard_map.147 = bf16[32,64,256]{2,1,0:T(8,128)(2,1)} custom-call(bf16[32,64,256]{2,1,0:T(8,128)(2,1)} %bitcast.10), custom_call_target="tpu_custom_call" | custom-call | tf_op jit(solution)/shard_map/pallas_call | solution.py:101
  78.7 38.5 %shard_map.148 = bf16[2048,256]{1,0:T(8,128)(2,1)} custom-call(bf16[2048,256]{1,0:T(8,128)(2,1)} %bitcast.7, s32[1,2048]{1,0:T(1,128)} %get-tuple-element.18.slot_row_ref, s32[1,1024]{1,0:T(1,128)} %bitcast.13, bf16[256,768]{1,0:T(8,128)(2,1)} %w_qkv_ref.1), custom_call_target="tpu_custom_call" | custom-call | tf_op jit(solution)/shard_map/pallas_call | solution.py:381
  117.1 30.0 %shard_map.149 = bf16[32,64,256]{2,1,0:T(8,128)(2,1)} custom-call(bf16[32,64,256]{2,1,0:T(8,128)(2,1)} %bitcast.8), custom_call_target="tpu_custom_call" | custom-call | tf_op jit(solution)/shard_map/pallas_call | solution.py:101
  147.1 10.4 %shard_map.150 = f32[13,1024]{1,0:T(8,128)} custom-call(bf16[1024,256]{1,0:T(8,128)(2,1)} %get-tuple-element.16.x_ref, bf16[2048,256]{1,0:T(8,128)(2,1)} %bitcast.9, s32[1,1024]{1,0:T(1,128)} %get-tuple-element.15.pos_ref, bf16[256,256]{1,0:T(8,128)(2,1)} %w_out_ref.1, bf16[256,1024]{1,0:T(8,128)(2,1)} %w_up_ref.1, bf16[1024,256]{1,0:T(8,128)(2,1)} %w_down_ref.1, ...), custom_call_target="tpu_custom_call" | custom-call | tf_op jit(solution)/shard_map/pallas_call | solution.py:396

commit v3 on v2

v3 whole, which is shorter than its diff:
```python
import functools

import jax
import jax.numpy as jnp
from jax import lax
from jax.experimental import pallas as pl
from jax.experimental.pallas import tpu as pltpu
from jax.sharding import PartitionSpec as P

HEADS = 16
PATCH = 1024
REACH = 256
QUERY_BLOCK = 256
AXES = ("row", "col")
BF = jnp.bfloat16
F32 = jnp.float32
I32 = jnp.int32
VM = pl.BlockSpec(memory_space=pltpu.VMEM)


def dot(a, b):
    return jnp.dot(a, b, preferred_element_type=F32)


def dot_nt(a, b):
    return lax.dot_general(a, b, (((1,), (1,)), ((), ())), preferred_element_type=F32)


def layer_norm(values):
    center = values - jnp.mean(values, axis=-1, keepdims=True)
    spread = jnp.mean(center * center, axis=-1, keepdims=True)
    return center * lax.rsqrt(spread + 1e-05)


def pick(index, rows, cols, dim):
    grid = lax.broadcasted_iota(I32, (rows, cols), dim)
    return jnp.where(grid == index, 1.0, 0.0).astype(BF)


def column(row):
    return jnp.broadcast_to(row, (128, row.shape[1])).T[:, :1]


def place(device):
    inner = lax.axis_size("col")
    return (device // inner, device % inner)


def greet(me, devices):
    barrier = pltpu.get_barrier_semaphore()

    def signal(k, carry):
        pl.semaphore_signal(
            barrier, inc=1, device_id=place((me + k) % devices),
            device_id_type=pl.DeviceIdType.MESH,
        )
        return carry

    lax.fori_loop(1, devices, signal, 0)
    return lambda: pl.semaphore_wait(barrier, devices - 1)


def ship(src, dst, send_sem, recv_sem, device):
    return pltpu.make_async_remote_copy(
        src_ref=src, dst_ref=dst, send_sem=send_sem, recv_sem=recv_sem,
        device_id=place(device), device_id_type=pl.DeviceIdType.MESH,
    )


def spread(src_ref, dst_ref, send_sems, recv_sems, me, devices):
    def start(k, carry):
        peer = (me + k) % devices
        ship(
            src_ref.at[peer], dst_ref.at[me], send_sems.at[peer], recv_sems.at[me], peer
        ).start()
        return carry

    lax.fori_loop(1, devices, start, 0)


def gather_in(src_ref, dst_ref, send_sems, recv_sems, me, devices):
    def finish(k, carry):
        peer = (me + k) % devices
        ship(
            src_ref.at[peer], dst_ref.at[peer], send_sems.at[peer], recv_sems.at[peer], peer
        ).wait()
        return carry

    lax.fori_loop(1, devices, finish, 0)


def encode_kernel(
    devices, capacity, margin,
    z_ref, coarse_ref, fine_ref, parent_ref, nbr_ref,
    w_parent_ref, w_skip_ref, taps_ref, w_cpe_ref,
    x_ref, pos_ref, got_ref, recv_ref,
    slot_ref, take_ref, par_ref, edge_ref, edge_parent_ref, skip_ref, feat_ref, send_ref,
    send_sems, recv_sems, feat_send_sems, feat_recv_sems, send_side, recv_side,
):
    me = lax.axis_index(AXES)
    entered = greet(me, devices)
    rows = z_ref.shape[1]
    coarse_rows = coarse_ref.shape[0]
    coarse = par_ref.shape[0]
    block = 256
    par_ref[margin : margin + coarse_rows, :] = jax.nn.gelu(
        layer_norm(dot(coarse_ref[...], w_parent_ref[...]))
    ).astype(BF)

    z = z_ref[...]
    dest = z // rows
    slot = z % rows
    onehot = pick(dest, devices, rows, 0)
    earlier = lax.broadcasted_iota(I32, (rows, rows), 0) < lax.broadcasted_iota(I32, (rows, rows), 1)
    ahead = dot(onehot, jnp.where(earlier, 1.0, 0.0).astype(BF))
    rank = jnp.sum(ahead * onehot.astype(F32), axis=0, keepdims=True).astype(I32)
    pos = dest * capacity + rank
    pos_ref[...] = pos

    entered()
    after, before = (me + 1) % devices, (me + devices - 1) % devices
    moves = [
        ship(
            par_ref.at[pl.ds(coarse_rows, margin), :], par_ref.at[pl.ds(0, margin), :],
            send_side.at[0], recv_side.at[0], after,
        ),
        ship(
            par_ref.at[pl.ds(margin, margin), :],
            par_ref.at[pl.ds(margin + coarse_rows, margin), :],
            send_side.at[1], recv_side.at[1], before,
        ),
        ship(
            parent_ref.at[:, pl.ds(rows - REACH, REACH)], edge_parent_ref.at[0],
            send_side.at[2], recv_side.at[2], after,
        ),
        ship(
            parent_ref.at[:, pl.ds(0, REACH)], edge_parent_ref.at[1],
            send_side.at[3], recv_side.at[3], before,
        ),
        ship(
            fine_ref.at[pl.ds(rows - REACH, REACH), :], edge_ref.at[0],
            send_side.at[4], recv_side.at[4], after,
        ),
        ship(
            fine_ref.at[pl.ds(0, REACH), :], edge_ref.at[1],
            send_side.at[5], recv_side.at[5], before,
        ),
    ]
    for move in moves:
        move.start()

    code = slot + 1
    part = lax.broadcasted_iota(I32, (16, rows), 0)
    digits = jnp.where(part == 0, code // 32, jnp.where(part == 1, code % 32, 0))
    digits = digits.astype(F32).astype(BF)
    total = devices * capacity
    step = min(512, total)
    for start in range(0, total, step):
        got = dot_nt(digits, pick(pos - start, step, rows, 0)).astype(I32)
        got = got[0:1] * 32 + got[1:2] - 1
        for d in range(step // capacity):
            slot_ref[start // capacity + d] = got[:, d * capacity : (d + 1) * capacity]
    spread(slot_ref, take_ref, send_sems, recv_sems, me, devices)
    take_ref[me] = slot_ref[me]

    def skips(i, carry):
        at = pl.ds(pl.multiple_of(i * block, block), block)
        skip_ref[at, :] = jax.nn.gelu(layer_norm(dot(fine_ref[at, :], w_skip_ref[...])))
        return carry

    lax.fori_loop(0, rows // block, skips, 0)
    base_row = me * coarse_rows - margin
    for move in moves:
        move.wait()

    for side, start in ((0, 0), (1, REACH + rows)):
        chosen = dot(
            pick(column(edge_parent_ref[side] - base_row), REACH, coarse, 1), par_ref[...]
        )
        skip = jax.nn.gelu(layer_norm(dot(edge_ref[side], w_skip_ref[...])))
        feat_ref[start : start + REACH, :] = (chosen + skip).astype(BF)

    def join(i, carry):
        base = pl.multiple_of(i * block, block)
        at = pl.ds(base, block)
        chosen = dot(pick(column(parent_ref[:, at] - base_row), block, coarse, 1), par_ref[...])
        feat_ref[pl.ds(base + REACH, block), :] = (chosen + skip_ref[at, :]).astype(BF)
        return carry

    lax.fori_loop(0, rows // block, join, 0)
    window = block + 2 * REACH

    def conv(i, carry):
        base = pl.multiple_of(i * block, block)
        at = pl.ds(base, block)
        cells = feat_ref[pl.ds(base, window), :]
        offsets = nbr_ref[:, at].T
        here = lax.broadcasted_iota(I32, offsets.shape, 0) + REACH
        source = jnp.where(offsets != REACH + 1, here + offsets, -1)
        acc = jnp.zeros((block, cells.shape[1]), F32)
        for t in range(nbr_ref.shape[0]):
            acc = acc + dot(pick(source[:, t : t + 1], block, window, 1), cells) * taps_ref[t : t + 1, :]
        out = layer_norm(dot(acc.astype(BF), w_cpe_ref[...]))
        center = feat_ref[pl.ds(base + REACH, block), :]
        x_ref[at, :] = (center.astype(F32) + out).astype(BF)
        return carry

    lax.fori_loop(0, rows // block, conv, 0)
    pos = pos_ref[...]
    per = block // capacity

    def pack(i, carry):
        sent = dot(pick(pos - i * block, block, rows, 0), x_ref[...]).astype(BF)
        send_ref[pl.ds(i * per, per)] = sent.reshape(per, capacity, sent.shape[1])
        return carry

    lax.fori_loop(0, devices // per, pack, 0)
    spread(send_ref, recv_ref, feat_send_sems, feat_recv_sems, me, devices)
    recv_ref[me] = send_ref[me]
    gather_in(slot_ref, take_ref, send_sems, recv_sems, me, devices)
    for d in range(devices):
        got_ref[:, d * capacity : (d + 1) * capacity] = take_ref[d]
    gather_in(send_ref, recv_ref, feat_send_sems, feat_recv_sems, me, devices)


def decode_kernel(
    devices, capacity, query_block,
    recv_ref, slot_row_ref, seg_ref, x_ref, pos_ref,
    w_qkv_ref, w_out_ref, w_up_ref, w_down_ref, w_cls_ref,
    out_ref,
    q_ref, k_ref, v_ref, fq_ref, fk_ref, acc_ref, home_ref, back_ref, ret_ref,
    send_sems, recv_sems,
):
    me = lax.axis_index(AXES)
    entered = greet(me, devices)
    rows, width = q_ref.shape
    total = recv_ref.shape[0]
    head_dim = width // HEADS
    lanes = 128
    per_group = lanes // head_dim
    block = 256

    def unpack(i, carry):
        at = pl.ds(pl.multiple_of(i * block, block), block)
        z = dot(pick(slot_row_ref[...] - i * block, block, total, 0), recv_ref[...])
        normed = layer_norm(z).astype(BF)
        qkv = dot(normed, w_qkv_ref[...])
        q_ref[at, :] = qkv[:, :width].astype(BF) * jnp.asarray(head_dim**-0.5, BF)
        k_ref[at, :] = qkv[:, width : 2 * width].astype(BF)
        v_ref[at, :] = qkv[:, 2 * width :].astype(BF)
        return carry

    lax.fori_loop(0, rows // block, unpack, 0)
    bits = (PATCH - 1).bit_length()
    lane = lax.broadcasted_iota(I32, (rows, lanes), 1)
    seg = jnp.broadcast_to(seg_ref[...] - seg_ref[:, 0:1], (lanes, rows)).T
    code = ((seg >> (lane // 2)) & 1) ^ (lane & 1)
    used = lane < 2 * bits
    fq_ref[...] = jnp.where(used & (code == 1), 1.0, 0.0).astype(BF)
    fk_ref[...] = jnp.where(used & (code == 0), -1e30, 0.0).astype(BF)
    owner = lane // head_dim
    per = block // capacity
    groups = width // lanes

    for g in range(groups):
        cols = slice(g * lanes, (g + 1) * lanes)
        acc_ref[...] = jnp.zeros_like(acc_ref)

        def head(h, carry):
            mine = owner == h
            keys = jnp.where(mine, k_ref[:, cols], jnp.zeros((), BF))
            keys = jnp.concatenate([keys, fk_ref[...]], axis=1)
            values = jnp.where(mine, v_ref[:, cols], jnp.zeros((), BF))
            values = jnp.concatenate([values, jnp.ones((rows, lanes), BF)], axis=1)
            for start in range(0, rows, query_block):
                at = slice(start, start + query_block)
                query = jnp.concatenate([q_ref[at, cols], fq_ref[at, :]], axis=1)
                scores = dot_nt(query, keys)
                top = jnp.max(scores, axis=-1, keepdims=True)
                probs = jnp.exp(scores - top).astype(BF)
                out = dot(probs, values)
                acc_ref[at, :] += out[:, :lanes] / out[:, lanes:]
            return carry

        lax.fori_loop(0, per_group, head, 0)
        home_ref[:, cols] = acc_ref[...].astype(BF)

        def pack(i, carry):
            at = pl.ds(pl.multiple_of(i * block, block), block)
            sent = dot(pick(column(slot_row_ref[:, at]), block, rows, 1), home_ref[:, cols])
            back_ref[g, pl.ds(i * per, per)] = sent.astype(BF).reshape(per, capacity, lanes)
            return carry

        lax.fori_loop(0, devices // per, pack, 0)
        if g == 0:
            entered()
        spread(back_ref.at[g], ret_ref.at[g], send_sems.at[g], recv_sems.at[g], me, devices)
        ret_ref[g, me] = back_ref[g, me]

    for g in range(groups):
        cols = slice(g * lanes, (g + 1) * lanes)
        gather_in(back_ref.at[g], ret_ref.at[g], send_sems.at[g], recv_sems.at[g], me, devices)
        returned = ret_ref[g].reshape(total, lanes)
        for start in range(0, rows, block):
            at = slice(start, start + block)
            home = dot(pick(column(pos_ref[:, at]), block, total, 1), returned)
            home_ref[at, cols] = home.astype(BF)

    for start in range(0, rows, block):
        at = slice(start, start + block)
        o = dot(home_ref[at, :], w_out_ref[...]).astype(BF)
        x_two = x_ref[at, :].astype(F32) + o.astype(F32)
        hidden = jax.nn.gelu(dot(layer_norm(x_two).astype(BF), w_up_ref[...])).astype(BF)
        x_three = x_two + dot(hidden, w_down_ref[...])
        out_ref[:, at] = dot_nt(w_cls_ref[...], layer_norm(x_three).astype(BF))


def local(
    coarse_feats,
    fine_feats,
    parent_index,
    nbr_offset,
    z_position,
    segment_id,
    w_parent,
    w_skip,
    conv_taps,
    w_cpe,
    w_qkv,
    w_out,
    w_up,
    w_down,
    w_cls,
):
    fine_rows, width = fine_feats.shape
    coarse_rows = coarse_feats.shape[0]
    devices = lax.axis_size(AXES)
    capacity = 2 * fine_rows // devices
    total = devices * capacity
    assert fine_rows == PATCH

    fine_per_coarse = fine_rows // coarse_rows
    margin = coarse_rows // 2 + REACH // fine_per_coarse
    lanes = 128
    groups = width // lanes
    pair = pltpu.SemaphoreType.DMA((devices,))
    x_feats, pos, slots, recv = pl.pallas_call(
        functools.partial(encode_kernel, devices, capacity, margin),
        out_shape=(
            jax.ShapeDtypeStruct((fine_rows, width), BF),
            jax.ShapeDtypeStruct((1, fine_rows), I32),
            jax.ShapeDtypeStruct((1, total), I32),
            jax.ShapeDtypeStruct((devices, capacity, width), BF),
        ),
        in_specs=[VM] * 9,
        out_specs=(VM,) * 4,
        scratch_shapes=[
            pltpu.VMEM((devices, 1, capacity), I32),
            pltpu.VMEM((devices, 1, capacity), I32),
            pltpu.VMEM((coarse_rows + 2 * margin, width), BF),
            pltpu.VMEM((2, REACH, width), BF),
            pltpu.VMEM((2, 1, REACH), I32),
            pltpu.VMEM((fine_rows, width), F32),
            pltpu.VMEM((fine_rows + 2 * REACH, width), BF),
            pltpu.VMEM((devices, capacity, width), BF),
            pair, pair, pair, pair,
            pltpu.SemaphoreType.DMA((6,)),
            pltpu.SemaphoreType.DMA((6,)),
        ],
        compiler_params=pltpu.CompilerParams(collective_id=0, has_side_effects=True),
    )(
        z_position.reshape(1, fine_rows), coarse_feats, fine_feats,
        parent_index.reshape(1, fine_rows), nbr_offset,
        w_parent, w_skip, conv_taps, w_cpe,
    )
    return pl.pallas_call(
        functools.partial(decode_kernel, devices, capacity, QUERY_BLOCK),
        out_shape=jax.ShapeDtypeStruct((w_cls.shape[0], fine_rows), F32),
        in_specs=[VM] * 10,
        out_specs=VM,
        scratch_shapes=[
            pltpu.VMEM((fine_rows, width), BF),
            pltpu.VMEM((fine_rows, width), BF),
            pltpu.VMEM((fine_rows, width), BF),
            pltpu.VMEM((fine_rows, lanes), BF),
            pltpu.VMEM((fine_rows, lanes), BF),
            pltpu.VMEM((fine_rows, lanes), F32),
            pltpu.VMEM((fine_rows, width), BF),
            pltpu.VMEM((groups, devices, capacity, lanes), BF),
            pltpu.VMEM((groups, devices, capacity, lanes), BF),
            pltpu.SemaphoreType.DMA((groups, devices)),
            pltpu.SemaphoreType.DMA((groups, devices)),
        ],
        compiler_params=pltpu.CompilerParams(collective_id=1, has_side_effects=True),
    )(
        recv.reshape(total, width), slots, segment_id.reshape(1, fine_rows), x_feats, pos,
        w_qkv, w_out, w_up, w_down, w_cls,
    )


def solution(mesh):
    rows = P(AXES, None)
    flat = P(AXES)
    placed = (rows, rows, flat, P(None, AXES), flat, flat) + (P(),) * 9
    return jax.shard_map(
        local, mesh=mesh, in_specs=placed, out_specs=P(None, AXES), check_vma=False
    )
```

time: 158 us -> 131 us (0.83)
  Pallas kernels: 157 us -> 128 us
    pallas_call x6 -> x2, Pallas kernels: 157 us -> 128 us  [the longest x1 64.4 us: local(): pl.pallas_call(functools.partial(encode_kernel, devices, capacity, margin...]
where the time goes in v3:
time: 131 us; the launch traced here: 130 us
  Pallas kernels  128 us (98%)
  local copies, waits for them, and re-layouts  1.47 us (1%)
    pallas_call x1, Pallas kernels, local(): pl.pallas_call(functools.partial(encode_kernel, devices, capacity, margin...  64.4 us
    pallas_call x1, Pallas kernels, local(): pl.pallas_call(functools.partial(decode_kernel, devices, capacity, QUERY_...  63.9 us

profile of v3, /device:TPU:0, one launch (start us, length us, event | category | flops | bytes accessed | tf_op | source)
XLA Modules:
  0.0 129.8 jit_solution(11797787099175528130)
XLA Ops:
  0.0 64.4 %shard_map.145 = (bf16[1024,256]{1,0:T(8,128)(2,1)}, s32[1,1024]{1,0:T(1,128)}, s32[1,2048]{1,0:T(1,128)}, bf16[32,64,256]{2,1,0:T(8,128)(2,1)}) custom-call(s32[1,1024]{1,0:T(1,128)} %bitcast.5, bf16[256,512]{1,0:T(8,128)(2,1)} %coarse_ref.1, bf16[1024,256]{1,0:T(8,128)(2,1)} %fine_ref.1, s32[1,1024]{1,0:T(1,128)} %bitcast.6, s32[27,1024]{1,0:T(8,128)} %nbr_ref.1, ...), custom_call_target="tpu_custom_call" | custom-call | tf_op jit(solution)/shard_map/pallas_call | solution.py:347
  64.4 63.9 %shard_map.146 = f32[13,1024]{1,0:T(8,128)} custom-call(bf16[2048,256]{1,0:T(8,128)(2,1)} %bitcast.4, s32[1,2048]{1,0:T(1,128)} %get-tuple-element.10.slot_row_ref, s32[1,1024]{1,0:T(1,128)} %bitcast.7, bf16[1024,256]{1,0:T(8,128)(2,1)} %get-tuple-element.11.x_ref, s32[1,1024]{1,0:T(1,128)} %get-tuple-element.12.pos_ref, bf16[256,768]{1,0:T(8,128)(2,1)} %w_qkv_ref.1, ...), custom_call_target="tpu_custom_call" | custom-call | tf_op jit(solution)/shard_map/pallas_call | solution.py:376
  128.3 1.5 %copy.17 = f32[13,1024]{1,0:T(8,128)} copy(f32[13,1024]{1,0:T(8,128)} %shard_map.146) | data formatting | bytes 106496

commit v4 on v3

--- a/solution.py
+++ b/solution.py
@@ -10,7 +10,7 @@
 HEADS = 16
 PATCH = 1024
 REACH = 256
-QUERY_BLOCK = 256
+QUERY_BLOCK = 512
 AXES = ("row", "col")
 BF = jnp.bfloat16
 F32 = jnp.float32
@@ -33,8 +33,10 @@
 
 
 def pick(index, rows, cols, dim):
-    grid = lax.broadcasted_iota(I32, (rows, cols), dim)
-    return jnp.where(grid == index, 1.0, 0.0).astype(BF)
+    shape = (rows, cols)
+    grid = lax.broadcasted_iota(I32, shape, dim).astype(jnp.int16)
+    want = jnp.broadcast_to(jnp.clip(index, -1, 32767), shape).astype(jnp.int16)
+    return jnp.where(grid == want, jnp.ones((), BF), jnp.zeros((), BF))
 
 
 def column(row):

time: 131 us -> 133 us (1.015)
  Pallas kernels: 128 us -> 130 us
    pallas_call x1, Pallas kernels: 63.9 us -> 66.3 us  [local(): pl.pallas_call(functools.partial(decode_kernel, devices, capacity, QUERY_...]
where the time goes in v4:
time: 133 us; the launch traced here: 132 us
  Pallas kernels  130 us (98%)
  local copies, waits for them, and re-layouts  1.47 us (1%)
    pallas_call x1, Pallas kernels, local(): pl.pallas_call(functools.partial(decode_kernel, devices, capacity, QUERY_...  66.3 us
    pallas_call x1, Pallas kernels, local(): pl.pallas_call(functools.partial(encode_kernel, devices, capacity, margin...  64.1 us

profile of v4, /device:TPU:0, one launch (start us, length us, event | category | flops | bytes accessed | tf_op | source)
XLA Modules:
  0.0 131.9 jit_solution(5054382654130328517)
XLA Ops:
  0.0 64.1 %shard_map.145 = (bf16[1024,256]{1,0:T(8,128)(2,1)}, s32[1,1024]{1,0:T(1,128)}, s32[1,2048]{1,0:T(1,128)}, bf16[32,64,256]{2,1,0:T(8,128)(2,1)}) custom-call(s32[1,1024]{1,0:T(1,128)} %bitcast.5, bf16[256,512]{1,0:T(8,128)(2,1)} %coarse_ref.1, bf16[1024,256]{1,0:T(8,128)(2,1)} %fine_ref.1, s32[1,1024]{1,0:T(1,128)} %bitcast.6, s32[27,1024]{1,0:T(8,128)} %nbr_ref.1, ...), custom_call_target="tpu_custom_call" | custom-call | tf_op jit(solution)/shard_map/pallas_call | solution.py:349
  64.1 66.3 %shard_map.146 = f32[13,1024]{1,0:T(8,128)} custom-call(bf16[2048,256]{1,0:T(8,128)(2,1)} %bitcast.4, s32[1,2048]{1,0:T(1,128)} %get-tuple-element.10.slot_row_ref, s32[1,1024]{1,0:T(1,128)} %bitcast.7, bf16[1024,256]{1,0:T(8,128)(2,1)} %get-tuple-element.11.x_ref, s32[1,1024]{1,0:T(1,128)} %get-tuple-element.12.pos_ref, bf16[256,768]{1,0:T(8,128)(2,1)} %w_qkv_ref.1, ...), custom_call_target="tpu_custom_call" | custom-call | tf_op jit(solution)/shard_map/pallas_call | solution.py:378
  130.4 1.5 %copy.17 = f32[13,1024]{1,0:T(8,128)} copy(f32[13,1024]{1,0:T(8,128)} %shard_map.146) | data formatting | bytes 106496
